TPU v7x, 512 devices: a whole 4x4x16 slice. The times are simulated.
512 devices in a mesh: dp: 4 (over x), context: 16 (over z_lo, core), head: 8 (over y, z_hi).
Axes of the slice: x: 4, y: 4, z: 16 (z_hi: 2, z_lo: 8; z = z_hi * 8 + z_lo), core: 2. Of those that a mesh axis runs over, the one named last changes fastest.
Arguments:
- hidden: bfloat16 [4, 3072, 4096], P('dp', 'context'), may hold values from -6 to 6
- queries: bfloat16 [4, 3072, 4096], P('dp', 'context', 'head'), may hold values from -216 to 216
- grad_out: bfloat16 [4, 3072, 4096], P('dp', 'context', 'head'), may hold values from -6 to 6
- segment: int32 [4, 3072], P('dp', 'context'), may hold values from 0 to 3, never falling along the last dimension, each value on 1 to 1920 neighbouring positions
- key_proj: bfloat16 [4096, 1024], P(('dp', 'context'), 'head'), may hold values from -0.09375 to 0.09375
- value_proj: bfloat16 [4096, 1024], P(('dp', 'context'), 'head'), may hold values from -0.09375 to 0.09375
Outputs:
- grad_queries: bfloat16 [4, 3072, 4096], P('dp', 'context', 'head')
- grad_key_proj: float32 [4096, 1024], P(('dp', 'context'), 'head')
- grad_value_proj: float32 [4096, 1024], P(('dp', 'context'), 'head')
Inputs may be any that keep to these rules, and one draw needn't show every extreme that they name: segment ids never fall along a trace; each trace has 4 segments, one of exactly 1920 tokens.
All inputs are finite; a program needn't handle non-finite values.
Results may differ from a plain program's by a relative error of at most 0.04.
The roundings to bfloat16 on the way count: a program that leaves them out, or rounds other values in their place, can miss the bound.
Values may be sent and summed in bfloat16 or wider, within the bound.
A program may use at most 64 MiB of HBM per device.

v0:
```python
import jax
import jax.numpy as jnp
from jax import lax
from jax.sharding import PartitionSpec as P

HEADS = 32
KV_HEADS = 8
HEAD_DIM = 128
far_below = -1e30


def passed_along(block, axis, distance):
    devices = range(lax.axis_size(axis))
    route = [((i - distance) % len(devices), i) for i in devices]
    return lax.ppermute(block, axis, route)


def body(hidden, queries, grad_out, segment, key_proj, value_proj):
    tok_rows = hidden.shape[1]
    local_rows = hidden[0]
    kv_local = key_proj.shape[1] // HEAD_DIM
    group = HEADS // KV_HEADS
    scale = HEAD_DIM ** (-0.5)
    steps = lax.axis_size("context")
    pieces = (
        lax.all_gather(key_proj, ("dp", "context"), axis=0, tiled=True),
        lax.all_gather(value_proj, ("dp", "context"), axis=0, tiled=True),
    )
    columns = local_rows
    key_sum = jnp.dot(columns, pieces[0], preferred_element_type=jnp.float32)
    value_sum = jnp.dot(columns, pieces[1], preferred_element_type=jnp.float32)
    keys = key_sum.astype(jnp.bfloat16).reshape(tok_rows, kv_local, HEAD_DIM)
    values = value_sum.astype(jnp.bfloat16).reshape(tok_rows, kv_local, HEAD_DIM)
    marks = segment[0].astype(jnp.bfloat16)
    query_heads = queries[0].reshape(tok_rows, kv_local, group, HEAD_DIM)
    cot_heads = grad_out[0].reshape(tok_rows, kv_local, group, HEAD_DIM)

    def masked_scores(key_part, mark_part):
        raw = (
            jnp.einsum("qhgd,khd->qhgk", query_heads, key_part, preferred_element_type=jnp.float32)
            * scale
        )
        same = (marks[:, None] == mark_part[None, :])[:, None, None, :]
        return (jnp.where(same, raw, far_below), same)

    buffers = ()
    stat_shape = (tok_rows, kv_local, group)
    pieces = (
        lax.all_gather(keys, "context", axis=0, tiled=True),
        lax.all_gather(values, "context", axis=0, tiled=True),
        lax.all_gather(marks, "context", axis=0, tiled=True),
    )
    top = jnp.full(stat_shape, far_below, jnp.float32)
    stored = buffers
    raw, same = masked_scores(pieces[0], pieces[2])
    new_top = jnp.maximum(top, jnp.max(raw, axis=-1))
    weights = jnp.where(same, jnp.exp(raw - new_top[..., None]), 0.0)
    total = jnp.sum(weights, axis=-1)
    acc = jnp.einsum(
        "qhgk,khd->qhgd",
        weights.astype(jnp.bfloat16),
        pieces[1],
        preferred_element_type=jnp.float32,
    )
    top, total, acc, stored = (new_top, total, acc, stored)
    output = (acc / total[..., None]).astype(jnp.bfloat16)
    log_total = top + jnp.log(total)
    delta = jnp.sum(cot_heads.astype(jnp.float32) * output.astype(jnp.float32), axis=-1)

    def visit(key_part, value_part, mark_part, query_acc):
        raw, same = masked_scores(key_part, mark_part)
        probs = jnp.where(same, jnp.exp(raw - log_total[..., None]), 0.0)
        probs_b = probs.astype(jnp.bfloat16)
        value_part_grad = jnp.einsum(
            "qhgk,qhgd->khd", probs_b, cot_heads, preferred_element_type=jnp.float32
        )
        prob_grad = jnp.einsum(
            "qhgd,khd->qhgk", cot_heads, value_part, preferred_element_type=jnp.float32
        )
        dscores = (probs * (prob_grad - delta[..., None])).astype(jnp.bfloat16)
        query_acc = (
            query_acc
            + jnp.einsum("qhgk,khd->qhgd", dscores, key_part, preferred_element_type=jnp.float32)
            * scale
        )
        key_part_grad = (
            jnp.einsum("qhgk,qhgd->khd", dscores, query_heads, preferred_element_type=jnp.float32)
            * scale
        )
        return (query_acc, key_part_grad, value_part_grad)

    zero_grads = jnp.zeros((tok_rows, kv_local, HEAD_DIM), jnp.float32)
    query_zero = jnp.zeros((tok_rows, kv_local, group, HEAD_DIM), jnp.float32)

    def turn(index, state):
        key_part, value_part, mark_part, key_grad, value_grad, query_acc = state
        query_acc, key_more, value_more = visit(key_part, value_part, mark_part, query_acc)
        key_part, value_part, mark_part = passed_along(
            (key_part, value_part, mark_part), "context", 1
        )
        key_grad, value_grad = passed_along(
            (key_grad + key_more, value_grad + value_more), "context", 1
        )
        return (key_part, value_part, mark_part, key_grad, value_grad, query_acc)

    state = lax.fori_loop(0, steps, turn, (keys, values, marks, zero_grads, zero_grads, query_zero))
    key_grad, value_grad, query_acc = (state[3], state[4], state[5])
    grad_queries = query_acc.astype(jnp.bfloat16).reshape(1, tok_rows, kv_local * group * HEAD_DIM)
    both_grads = jnp.concatenate(
        [
            key_grad.astype(jnp.bfloat16).reshape(tok_rows, kv_local * HEAD_DIM),
            value_grad.astype(jnp.bfloat16).reshape(tok_rows, kv_local * HEAD_DIM),
        ],
        1,
    )
    columns = local_rows
    summed = lax.psum_scatter(
        jnp.einsum("td,tc->dc", columns, both_grads, preferred_element_type=jnp.float32),
        ("dp", "context"),
        scatter_dimension=0,
        tiled=True,
    )
    width_kv = key_proj.shape[1]
    return (grad_queries, summed[:, :width_kv], summed[:, width_kv:])


def solution(mesh):
    placed = (
        P("dp", "context", None),
        P("dp", "context", "head"),
        P("dp", "context", "head"),
        P("dp", "context"),
        P(("dp", "context"), "head"),
        P(("dp", "context"), "head"),
    )
    return jax.shard_map(
        body,
        mesh=mesh,
        in_specs=placed,
        out_specs=(
            P("dp", "context", "head"),
            P(("dp", "context"), "head"),
            P(("dp", "context"), "head"),
        ),
        check_vma=False,
    )
```

profile of v0, /device:TPU:8, one launch (start us, length us, event | category | flops | bytes accessed | tf_op | source)
XLA Modules:
  0.0 1097.5 jit_solution(6544349401803940098)
XLA Ops:
  13.6 56.4 %all-reduce = bf16[3072]{0:T(1024)(128)(2,1)S(1)} all-reduce(bf16[3072]{0:T(1024)(128)(2,1)S(1)} %dynamic-update-slice), channel_id=2, replica_groups=mesh['dp'=4,'context'=16,'head'=8] {'context'}, use_global_device_ids=true, to_apply=%add | all-reduce | flops 3072 | bytes 12288
  71.5 62.4 %all-gather.6.cloned.1.call-done = bf16[4096,128]{1,0:T(8,128)(2,1)} async-done(((bf16[64,128]{1,0:T(8,128)(2,1)}), bf16[4096,128]{1,0:T(8,128)(2,1)}) %all-gather.6.cloned.1.call-update) | async-done | bytes 1048592 | tf_op jit(solution)/shard_map/all_gather | solution.py:26
  135.6 33.5 %all-gather.1 = bf16[3072,128]{1,0:T(8,128)(2,1)S(1)} all-gather(bf16[192,128]{1,0:T(8,128)(2,1)S(1)} %fusion.40), channel_id=3, replica_groups=mesh['dp'=4,'context'=16,'head'=8] {'context'}, dimensions={0}, use_global_device_ids=true | all-gather | bytes 835584 | tf_op jit(solution)/shard_map/all_gather | solution.py:49
  169.1 5.6 fusion.25
  174.7 76.3 %all-gather.8.cloned.1.call-done = bf16[4096,128]{1,0:T(8,128)(2,1)} async-done(((bf16[64,128]{1,0:T(8,128)(2,1)}), bf16[4096,128]{1,0:T(8,128)(2,1)}) %all-gather.8.cloned.1.call-update) | async-done | bytes 1048592 | tf_op jit(solution)/shard_map/all_gather | solution.py:27
  251.0 1.9 fusion.43
  252.9 33.5 %all-gather.2 = bf16[3072,128]{1,0:T(8,128)(2,1)S(1)} all-gather(bf16[192,128]{1,0:T(8,128)(2,1)S(1)} %fusion.43), channel_id=4, replica_groups=mesh['dp'=4,'context'=16,'head'=8] {'context'}, dimensions={0}, use_global_device_ids=true | all-gather | bytes 835584 | tf_op jit(solution)/shard_map/all_gather | solution.py:50
  286.4 6.5 fusion.27
  293.0 2.7 fusion.61
  295.7 346.3 %while.21 = (s32[]{:T(128)}, bf16[192,1,128]{2,0,1:T(8,128)(2,1)S(1)}, bf16[192,1,128]{2,0,1:T(8,128)(2,1)S(1)}, bf16[192]{0:T(256)(128)(2,1)S(1)}, f32[192,1,12...) while((s32[]{:T(128)}, ...), condition=%wide.region_4.5_spmd.clone, body=%wide.region_3.4_spmd.clone.sunk | while | flops 190328832 | bytes 6227287 | solution.py:106
  295.7 2.3 collective-permute-start
  299.9 1.9 collective-permute-start.2
  302.9 1.9 collective-permute-start.3
  307.4 3.9 collective-permute-done.2
  311.4 4.1 collective-permute-done.3
  315.4 2.2 collective-permute-done.4
  329.1 3.9 collective-permute-done.2
  333.0 4.1 collective-permute-done.3
  337.0 2.2 collective-permute-done.4
  350.7 3.9 collective-permute-done.2
  354.6 4.1 collective-permute-done.3
  358.7 2.2 collective-permute-done.4
  372.3 3.9 collective-permute-done.2
  376.2 4.1 collective-permute-done.3
  380.3 2.2 collective-permute-done.4
  393.9 3.9 collective-permute-done.2
  397.8 4.1 collective-permute-done.3
  401.9 2.2 collective-permute-done.4
  415.5 3.9 collective-permute-done.2
  419.5 4.1 collective-permute-done.3
  423.5 2.2 collective-permute-done.4
  437.2 3.9 collective-permute-done.2
  441.1 4.1 collective-permute-done.3
  445.1 2.2 collective-permute-done.4
  458.8 3.9 collective-permute-done.2
  462.7 4.1 collective-permute-done.3
  466.8 2.2 collective-permute-done.4
  480.4 3.9 collective-permute-done.2
  484.3 4.1 collective-permute-done.3
  488.4 2.2 collective-permute-done.4
  502.0 3.9 collective-permute-done.2
  505.9 4.1 collective-permute-done.3
  510.0 2.2 collective-permute-done.4
  523.6 3.9 collective-permute-done.2
  527.6 4.1 collective-permute-done.3
  531.6 2.2 collective-permute-done.4
  545.2 3.9 collective-permute-done.2
  549.2 4.1 collective-permute-done.3
  553.2 2.2 collective-permute-done.4
  566.9 3.9 collective-permute-done.2
  570.8 4.1 collective-permute-done.3
  574.9 2.2 collective-permute-done.4
  588.5 3.9 collective-permute-done.2
  592.4 4.1 collective-permute-done.3
  596.5 2.2 collective-permute-done.4
  610.1 3.9 collective-permute-done.2
  614.0 4.1 collective-permute-done.3
  618.1 2.2 collective-permute-done.4
  631.7 3.9 collective-permute-done.2
  635.7 4.1 collective-permute-done.3
  639.7 2.2 collective-permute-done.4
  641.9 2.7 convolution_bitcast_fusion.3
  644.7 5.6 copy.31
  651.2 438.3 %reduce-scatter.4.cloned.1.call-done = f32[64,256]{1,0:T(8,128)} async-done(((f32[4096,256]{1,0:T(8,128)}), f32[64,256]{1,0:T(8,128)}) %reduce-scatter.4.cloned.1.call-update) | async-done | bytes 65552
  (285 shorter events, 186.5 us)
Async XLA Ops:
  7.2 126.7 %all-gather.6.cloned.1.call-start = ((), (), s32[]{:S(2)}) async-start(), calls=%async_computation.1 | async-start | bytes 1064960 | tf_op jit(solution)/shard_map/all_gather | solution.py:26
  7.9 243.1 %all-gather.8.cloned.1.call-start = ((), (), s32[]{:S(2)}) async-start(), calls=%async_computation.2 | async-start | bytes 1064960 | tf_op jit(solution)/shard_map/all_gather | solution.py:27
  8.7 1080.9 %reduce-scatter.4.cloned.1.call-start = ((), (), s32[]{:S(2)}) async-start(), calls=%async_computation.3 | async-start | bytes 4259840
  295.7 15.7 %collective-permute-start = (bf16[192,1,128]{2,0,1:T(8,128)(2,1)S(1)}, bf16[192,1,128]{2,0,1:T(8,128)(2,1)S(1)}, u32[]{:S(2)}, u32[]{:S(2)}) collective-permute-start(bf16[192,1,128]{2,0,1:T(8,128)(2,1)S(1)} %copy.49), channel_id=1, source_target_pairs={{120,0},{0,8},{8,16},{16,24},{24,32},{32,40},{40,48},{48,56},{56,6... | collective-permute-start | bytes 147464 | tf_op jit(solution)/shard_map/while/body/eval_jaxpr/ppermute | solution.py:15
  298.0 13.4 %collective-permute-start.1 = (bf16[192,1,128]{2,0,1:T(8,128)(2,1)S(1)}, bf16[192,1,128]{2,0,1:T(8,128)(2,1)S(1)}, u32[]{:S(2)}, u32[]{:S(2)}) collective-permute-start(bf16[192,1,128]{2,0,1:T(8,128)(2,1)S(1)} %copy.50), channel_id=1, source_target_pairs={{120,0},{0,8},{8,16},{16,24},{24,32},{32,40},{40,48},{48,56},{56,6... | collective-permute-start | bytes 147464 | tf_op jit(solution)/shard_map/while/body/eval_jaxpr/ppermute | solution.py:15
  302.9 12.5 %collective-permute-start.3 = (f32[192,1,128]{2,0,1:T(8,128)S(1)}, f32[192,1,128]{2,0,1:T(8,128)S(1)}, u32[]{:S(2)}, u32[]{:S(2)}) collective-permute-start(f32[192,1,128]{2,0,1:T(8,128)S(1)} %fusion.107), channel_id=1, source_target_pairs={{120,0},{0,8},{8,16},{16,24},{24,32},{32,40},{40,48},{48,56},{56,6... | collective-permute-start | bytes 294920 | tf_op jit(solution)/shard_map/while/body/eval_jaxpr/ppermute | solution.py:15
  305.1 12.5 %collective-permute-start.4 = (f32[192,1,128]{2,0,1:T(8,128)S(1)}, f32[192,1,128]{2,0,1:T(8,128)S(1)}, u32[]{:S(2)}, u32[]{:S(2)}) collective-permute-start(f32[192,1,128]{2,0,1:T(8,128)S(1)} %fusion.108), channel_id=1, source_target_pairs={{120,0},{0,8},{8,16},{16,24},{24,32},{32,40},{40,48},{48,56},{56,6... | collective-permute-start | bytes 294920 | tf_op jit(solution)/shard_map/while/body/eval_jaxpr/ppermute | solution.py:15
  317.7 15.3 %collective-permute-start = (bf16[192,1,128]{2,0,1:T(8,128)(2,1)S(1)}, bf16[192,1,128]{2,0,1:T(8,128)(2,1)S(1)}, u32[]{:S(2)}, u32[]{:S(2)}) collective-permute-start(bf16[192,1,128]{2,0,1:T(8,128)(2,1)S(1)} %copy.49), channel_id=1, source_target_pairs={{120,0},{0,8},{8,16},{16,24},{24,32},{32,40},{40,48},{48,56},{56,6... | collective-permute-start | bytes 147464 | tf_op jit(solution)/shard_map/while/body/eval_jaxpr/ppermute | solution.py:15
  319.6 13.4 %collective-permute-start.1 = (bf16[192,1,128]{2,0,1:T(8,128)(2,1)S(1)}, bf16[192,1,128]{2,0,1:T(8,128)(2,1)S(1)}, u32[]{:S(2)}, u32[]{:S(2)}) collective-permute-start(bf16[192,1,128]{2,0,1:T(8,128)(2,1)S(1)} %copy.50), channel_id=1, source_target_pairs={{120,0},{0,8},{8,16},{16,24},{24,32},{32,40},{40,48},{48,56},{56,6... | collective-permute-start | bytes 147464 | tf_op jit(solution)/shard_map/while/body/eval_jaxpr/ppermute | solution.py:15
  324.5 12.5 %collective-permute-start.3 = (f32[192,1,128]{2,0,1:T(8,128)S(1)}, f32[192,1,128]{2,0,1:T(8,128)S(1)}, u32[]{:S(2)}, u32[]{:S(2)}) collective-permute-start(f32[192,1,128]{2,0,1:T(8,128)S(1)} %fusion.107), channel_id=1, source_target_pairs={{120,0},{0,8},{8,16},{16,24},{24,32},{32,40},{40,48},{48,56},{56,6... | collective-permute-start | bytes 294920 | tf_op jit(solution)/shard_map/while/body/eval_jaxpr/ppermute | solution.py:15
  326.7 12.5 %collective-permute-start.4 = (f32[192,1,128]{2,0,1:T(8,128)S(1)}, f32[192,1,128]{2,0,1:T(8,128)S(1)}, u32[]{:S(2)}, u32[]{:S(2)}) collective-permute-start(f32[192,1,128]{2,0,1:T(8,128)S(1)} %fusion.108), channel_id=1, source_target_pairs={{120,0},{0,8},{8,16},{16,24},{24,32},{32,40},{40,48},{48,56},{56,6... | collective-permute-start | bytes 294920 | tf_op jit(solution)/shard_map/while/body/eval_jaxpr/ppermute | solution.py:15
  339.3 15.3 %collective-permute-start = (bf16[192,1,128]{2,0,1:T(8,128)(2,1)S(1)}, bf16[192,1,128]{2,0,1:T(8,128)(2,1)S(1)}, u32[]{:S(2)}, u32[]{:S(2)}) collective-permute-start(bf16[192,1,128]{2,0,1:T(8,128)(2,1)S(1)} %copy.49), channel_id=1, source_target_pairs={{120,0},{0,8},{8,16},{16,24},{24,32},{32,40},{40,48},{48,56},{56,6... | collective-permute-start | bytes 147464 | tf_op jit(solution)/shard_map/while/body/eval_jaxpr/ppermute | solution.py:15
  341.2 13.4 %collective-permute-start.1 = (bf16[192,1,128]{2,0,1:T(8,128)(2,1)S(1)}, bf16[192,1,128]{2,0,1:T(8,128)(2,1)S(1)}, u32[]{:S(2)}, u32[]{:S(2)}) collective-permute-start(bf16[192,1,128]{2,0,1:T(8,128)(2,1)S(1)} %copy.50), channel_id=1, source_target_pairs={{120,0},{0,8},{8,16},{16,24},{24,32},{32,40},{40,48},{48,56},{56,6... | collective-permute-start | bytes 147464 | tf_op jit(solution)/shard_map/while/body/eval_jaxpr/ppermute | solution.py:15
  346.1 12.5 %collective-permute-start.3 = (f32[192,1,128]{2,0,1:T(8,128)S(1)}, f32[192,1,128]{2,0,1:T(8,128)S(1)}, u32[]{:S(2)}, u32[]{:S(2)}) collective-permute-start(f32[192,1,128]{2,0,1:T(8,128)S(1)} %fusion.107), channel_id=1, source_target_pairs={{120,0},{0,8},{8,16},{16,24},{24,32},{32,40},{40,48},{48,56},{56,6... | collective-permute-start | bytes 294920 | tf_op jit(solution)/shard_map/while/body/eval_jaxpr/ppermute | solution.py:15
  348.3 12.5 %collective-permute-start.4 = (f32[192,1,128]{2,0,1:T(8,128)S(1)}, f32[192,1,128]{2,0,1:T(8,128)S(1)}, u32[]{:S(2)}, u32[]{:S(2)}) collective-permute-start(f32[192,1,128]{2,0,1:T(8,128)S(1)} %fusion.108), channel_id=1, source_target_pairs={{120,0},{0,8},{8,16},{16,24},{24,32},{32,40},{40,48},{48,56},{56,6... | collective-permute-start | bytes 294920 | tf_op jit(solution)/shard_map/while/body/eval_jaxpr/ppermute | solution.py:15
  360.9 15.3 %collective-permute-start = (bf16[192,1,128]{2,0,1:T(8,128)(2,1)S(1)}, bf16[192,1,128]{2,0,1:T(8,128)(2,1)S(1)}, u32[]{:S(2)}, u32[]{:S(2)}) collective-permute-start(bf16[192,1,128]{2,0,1:T(8,128)(2,1)S(1)} %copy.49), channel_id=1, source_target_pairs={{120,0},{0,8},{8,16},{16,24},{24,32},{32,40},{40,48},{48,56},{56,6... | collective-permute-start | bytes 147464 | tf_op jit(solution)/shard_map/while/body/eval_jaxpr/ppermute | solution.py:15
  362.8 13.4 %collective-permute-start.1 = (bf16[192,1,128]{2,0,1:T(8,128)(2,1)S(1)}, bf16[192,1,128]{2,0,1:T(8,128)(2,1)S(1)}, u32[]{:S(2)}, u32[]{:S(2)}) collective-permute-start(bf16[192,1,128]{2,0,1:T(8,128)(2,1)S(1)} %copy.50), channel_id=1, source_target_pairs={{120,0},{0,8},{8,16},{16,24},{24,32},{32,40},{40,48},{48,56},{56,6... | collective-permute-start | bytes 147464 | tf_op jit(solution)/shard_map/while/body/eval_jaxpr/ppermute | solution.py:15
  367.7 12.5 %collective-permute-start.3 = (f32[192,1,128]{2,0,1:T(8,128)S(1)}, f32[192,1,128]{2,0,1:T(8,128)S(1)}, u32[]{:S(2)}, u32[]{:S(2)}) collective-permute-start(f32[192,1,128]{2,0,1:T(8,128)S(1)} %fusion.107), channel_id=1, source_target_pairs={{120,0},{0,8},{8,16},{16,24},{24,32},{32,40},{40,48},{48,56},{56,6... | collective-permute-start | bytes 294920 | tf_op jit(solution)/shard_map/while/body/eval_jaxpr/ppermute | solution.py:15
  370.0 12.5 %collective-permute-start.4 = (f32[192,1,128]{2,0,1:T(8,128)S(1)}, f32[192,1,128]{2,0,1:T(8,128)S(1)}, u32[]{:S(2)}, u32[]{:S(2)}) collective-permute-start(f32[192,1,128]{2,0,1:T(8,128)S(1)} %fusion.108), channel_id=1, source_target_pairs={{120,0},{0,8},{8,16},{16,24},{24,32},{32,40},{40,48},{48,56},{56,6... | collective-permute-start | bytes 294920 | tf_op jit(solution)/shard_map/while/body/eval_jaxpr/ppermute | solution.py:15
  382.5 15.3 %collective-permute-start = (bf16[192,1,128]{2,0,1:T(8,128)(2,1)S(1)}, bf16[192,1,128]{2,0,1:T(8,128)(2,1)S(1)}, u32[]{:S(2)}, u32[]{:S(2)}) collective-permute-start(bf16[192,1,128]{2,0,1:T(8,128)(2,1)S(1)} %copy.49), channel_id=1, source_target_pairs={{120,0},{0,8},{8,16},{16,24},{24,32},{32,40},{40,48},{48,56},{56,6... | collective-permute-start | bytes 147464 | tf_op jit(solution)/shard_map/while/body/eval_jaxpr/ppermute | solution.py:15
  384.4 13.4 %collective-permute-start.1 = (bf16[192,1,128]{2,0,1:T(8,128)(2,1)S(1)}, bf16[192,1,128]{2,0,1:T(8,128)(2,1)S(1)}, u32[]{:S(2)}, u32[]{:S(2)}) collective-permute-start(bf16[192,1,128]{2,0,1:T(8,128)(2,1)S(1)} %copy.50), channel_id=1, source_target_pairs={{120,0},{0,8},{8,16},{16,24},{24,32},{32,40},{40,48},{48,56},{56,6... | collective-permute-start | bytes 147464 | tf_op jit(solution)/shard_map/while/body/eval_jaxpr/ppermute | solution.py:15
  389.4 12.5 %collective-permute-start.3 = (f32[192,1,128]{2,0,1:T(8,128)S(1)}, f32[192,1,128]{2,0,1:T(8,128)S(1)}, u32[]{:S(2)}, u32[]{:S(2)}) collective-permute-start(f32[192,1,128]{2,0,1:T(8,128)S(1)} %fusion.107), channel_id=1, source_target_pairs={{120,0},{0,8},{8,16},{16,24},{24,32},{32,40},{40,48},{48,56},{56,6... | collective-permute-start | bytes 294920 | tf_op jit(solution)/shard_map/while/body/eval_jaxpr/ppermute | solution.py:15
  391.6 12.5 %collective-permute-start.4 = (f32[192,1,128]{2,0,1:T(8,128)S(1)}, f32[192,1,128]{2,0,1:T(8,128)S(1)}, u32[]{:S(2)}, u32[]{:S(2)}) collective-permute-start(f32[192,1,128]{2,0,1:T(8,128)S(1)} %fusion.108), channel_id=1, source_target_pairs={{120,0},{0,8},{8,16},{16,24},{24,32},{32,40},{40,48},{48,56},{56,6... | collective-permute-start | bytes 294920 | tf_op jit(solution)/shard_map/while/body/eval_jaxpr/ppermute | solution.py:15
  404.1 15.3 %collective-permute-start = (bf16[192,1,128]{2,0,1:T(8,128)(2,1)S(1)}, bf16[192,1,128]{2,0,1:T(8,128)(2,1)S(1)}, u32[]{:S(2)}, u32[]{:S(2)}) collective-permute-start(bf16[192,1,128]{2,0,1:T(8,128)(2,1)S(1)} %copy.49), channel_id=1, source_target_pairs={{120,0},{0,8},{8,16},{16,24},{24,32},{32,40},{40,48},{48,56},{56,6... | collective-permute-start | bytes 147464 | tf_op jit(solution)/shard_map/while/body/eval_jaxpr/ppermute | solution.py:15
  406.1 13.4 %collective-permute-start.1 = (bf16[192,1,128]{2,0,1:T(8,128)(2,1)S(1)}, bf16[192,1,128]{2,0,1:T(8,128)(2,1)S(1)}, u32[]{:S(2)}, u32[]{:S(2)}) collective-permute-start(bf16[192,1,128]{2,0,1:T(8,128)(2,1)S(1)} %copy.50), channel_id=1, source_target_pairs={{120,0},{0,8},{8,16},{16,24},{24,32},{32,40},{40,48},{48,56},{56,6... | collective-permute-start | bytes 147464 | tf_op jit(solution)/shard_map/while/body/eval_jaxpr/ppermute | solution.py:15
  411.0 12.5 %collective-permute-start.3 = (f32[192,1,128]{2,0,1:T(8,128)S(1)}, f32[192,1,128]{2,0,1:T(8,128)S(1)}, u32[]{:S(2)}, u32[]{:S(2)}) collective-permute-start(f32[192,1,128]{2,0,1:T(8,128)S(1)} %fusion.107), channel_id=1, source_target_pairs={{120,0},{0,8},{8,16},{16,24},{24,32},{32,40},{40,48},{48,56},{56,6... | collective-permute-start | bytes 294920 | tf_op jit(solution)/shard_map/while/body/eval_jaxpr/ppermute | solution.py:15
  413.2 12.5 %collective-permute-start.4 = (f32[192,1,128]{2,0,1:T(8,128)S(1)}, f32[192,1,128]{2,0,1:T(8,128)S(1)}, u32[]{:S(2)}, u32[]{:S(2)}) collective-permute-start(f32[192,1,128]{2,0,1:T(8,128)S(1)} %fusion.108), channel_id=1, source_target_pairs={{120,0},{0,8},{8,16},{16,24},{24,32},{32,40},{40,48},{48,56},{56,6... | collective-permute-start | bytes 294920 | tf_op jit(solution)/shard_map/while/body/eval_jaxpr/ppermute | solution.py:15
  425.7 15.3 %collective-permute-start = (bf16[192,1,128]{2,0,1:T(8,128)(2,1)S(1)}, bf16[192,1,128]{2,0,1:T(8,128)(2,1)S(1)}, u32[]{:S(2)}, u32[]{:S(2)}) collective-permute-start(bf16[192,1,128]{2,0,1:T(8,128)(2,1)S(1)} %copy.49), channel_id=1, source_target_pairs={{120,0},{0,8},{8,16},{16,24},{24,32},{32,40},{40,48},{48,56},{56,6... | collective-permute-start | bytes 147464 | tf_op jit(solution)/shard_map/while/body/eval_jaxpr/ppermute | solution.py:15
  427.7 13.4 %collective-permute-start.1 = (bf16[192,1,128]{2,0,1:T(8,128)(2,1)S(1)}, bf16[192,1,128]{2,0,1:T(8,128)(2,1)S(1)}, u32[]{:S(2)}, u32[]{:S(2)}) collective-permute-start(bf16[192,1,128]{2,0,1:T(8,128)(2,1)S(1)} %copy.50), channel_id=1, source_target_pairs={{120,0},{0,8},{8,16},{16,24},{24,32},{32,40},{40,48},{48,56},{56,6... | collective-permute-start | bytes 147464 | tf_op jit(solution)/shard_map/while/body/eval_jaxpr/ppermute | solution.py:15
  432.6 12.5 %collective-permute-start.3 = (f32[192,1,128]{2,0,1:T(8,128)S(1)}, f32[192,1,128]{2,0,1:T(8,128)S(1)}, u32[]{:S(2)}, u32[]{:S(2)}) collective-permute-start(f32[192,1,128]{2,0,1:T(8,128)S(1)} %fusion.107), channel_id=1, source_target_pairs={{120,0},{0,8},{8,16},{16,24},{24,32},{32,40},{40,48},{48,56},{56,6... | collective-permute-start | bytes 294920 | tf_op jit(solution)/shard_map/while/body/eval_jaxpr/ppermute | solution.py:15
  434.8 12.5 %collective-permute-start.4 = (f32[192,1,128]{2,0,1:T(8,128)S(1)}, f32[192,1,128]{2,0,1:T(8,128)S(1)}, u32[]{:S(2)}, u32[]{:S(2)}) collective-permute-start(f32[192,1,128]{2,0,1:T(8,128)S(1)} %fusion.108), channel_id=1, source_target_pairs={{120,0},{0,8},{8,16},{16,24},{24,32},{32,40},{40,48},{48,56},{56,6... | collective-permute-start | bytes 294920 | tf_op jit(solution)/shard_map/while/body/eval_jaxpr/ppermute | solution.py:15
  447.4 15.3 %collective-permute-start = (bf16[192,1,128]{2,0,1:T(8,128)(2,1)S(1)}, bf16[192,1,128]{2,0,1:T(8,128)(2,1)S(1)}, u32[]{:S(2)}, u32[]{:S(2)}) collective-permute-start(bf16[192,1,128]{2,0,1:T(8,128)(2,1)S(1)} %copy.49), channel_id=1, source_target_pairs={{120,0},{0,8},{8,16},{16,24},{24,32},{32,40},{40,48},{48,56},{56,6... | collective-permute-start | bytes 147464 | tf_op jit(solution)/shard_map/while/body/eval_jaxpr/ppermute | solution.py:15
  449.3 13.4 %collective-permute-start.1 = (bf16[192,1,128]{2,0,1:T(8,128)(2,1)S(1)}, bf16[192,1,128]{2,0,1:T(8,128)(2,1)S(1)}, u32[]{:S(2)}, u32[]{:S(2)}) collective-permute-start(bf16[192,1,128]{2,0,1:T(8,128)(2,1)S(1)} %copy.50), channel_id=1, source_target_pairs={{120,0},{0,8},{8,16},{16,24},{24,32},{32,40},{40,48},{48,56},{56,6... | collective-permute-start | bytes 147464 | tf_op jit(solution)/shard_map/while/body/eval_jaxpr/ppermute | solution.py:15
  454.2 12.5 %collective-permute-start.3 = (f32[192,1,128]{2,0,1:T(8,128)S(1)}, f32[192,1,128]{2,0,1:T(8,128)S(1)}, u32[]{:S(2)}, u32[]{:S(2)}) collective-permute-start(f32[192,1,128]{2,0,1:T(8,128)S(1)} %fusion.107), channel_id=1, source_target_pairs={{120,0},{0,8},{8,16},{16,24},{24,32},{32,40},{40,48},{48,56},{56,6... | collective-permute-start | bytes 294920 | tf_op jit(solution)/shard_map/while/body/eval_jaxpr/ppermute | solution.py:15
  456.4 12.5 %collective-permute-start.4 = (f32[192,1,128]{2,0,1:T(8,128)S(1)}, f32[192,1,128]{2,0,1:T(8,128)S(1)}, u32[]{:S(2)}, u32[]{:S(2)}) collective-permute-start(f32[192,1,128]{2,0,1:T(8,128)S(1)} %fusion.108), channel_id=1, source_target_pairs={{120,0},{0,8},{8,16},{16,24},{24,32},{32,40},{40,48},{48,56},{56,6... | collective-permute-start | bytes 294920 | tf_op jit(solution)/shard_map/while/body/eval_jaxpr/ppermute | solution.py:15
  469.0 15.3 %collective-permute-start = (bf16[192,1,128]{2,0,1:T(8,128)(2,1)S(1)}, bf16[192,1,128]{2,0,1:T(8,128)(2,1)S(1)}, u32[]{:S(2)}, u32[]{:S(2)}) collective-permute-start(bf16[192,1,128]{2,0,1:T(8,128)(2,1)S(1)} %copy.49), channel_id=1, source_target_pairs={{120,0},{0,8},{8,16},{16,24},{24,32},{32,40},{40,48},{48,56},{56,6... | collective-permute-start | bytes 147464 | tf_op jit(solution)/shard_map/while/body/eval_jaxpr/ppermute | solution.py:15
  470.9 13.4 %collective-permute-start.1 = (bf16[192,1,128]{2,0,1:T(8,128)(2,1)S(1)}, bf16[192,1,128]{2,0,1:T(8,128)(2,1)S(1)}, u32[]{:S(2)}, u32[]{:S(2)}) collective-permute-start(bf16[192,1,128]{2,0,1:T(8,128)(2,1)S(1)} %copy.50), channel_id=1, source_target_pairs={{120,0},{0,8},{8,16},{16,24},{24,32},{32,40},{40,48},{48,56},{56,6... | collective-permute-start | bytes 147464 | tf_op jit(solution)/shard_map/while/body/eval_jaxpr/ppermute | solution.py:15
  475.8 12.5 %collective-permute-start.3 = (f32[192,1,128]{2,0,1:T(8,128)S(1)}, f32[192,1,128]{2,0,1:T(8,128)S(1)}, u32[]{:S(2)}, u32[]{:S(2)}) collective-permute-start(f32[192,1,128]{2,0,1:T(8,128)S(1)} %fusion.107), channel_id=1, source_target_pairs={{120,0},{0,8},{8,16},{16,24},{24,32},{32,40},{40,48},{48,56},{56,6... | collective-permute-start | bytes 294920 | tf_op jit(solution)/shard_map/while/body/eval_jaxpr/ppermute | solution.py:15
  478.1 12.5 %collective-permute-start.4 = (f32[192,1,128]{2,0,1:T(8,128)S(1)}, f32[192,1,128]{2,0,1:T(8,128)S(1)}, u32[]{:S(2)}, u32[]{:S(2)}) collective-permute-start(f32[192,1,128]{2,0,1:T(8,128)S(1)} %fusion.108), channel_id=1, source_target_pairs={{120,0},{0,8},{8,16},{16,24},{24,32},{32,40},{40,48},{48,56},{56,6... | collective-permute-start | bytes 294920 | tf_op jit(solution)/shard_map/while/body/eval_jaxpr/ppermute | solution.py:15
  490.6 15.3 %collective-permute-start = (bf16[192,1,128]{2,0,1:T(8,128)(2,1)S(1)}, bf16[192,1,128]{2,0,1:T(8,128)(2,1)S(1)}, u32[]{:S(2)}, u32[]{:S(2)}) collective-permute-start(bf16[192,1,128]{2,0,1:T(8,128)(2,1)S(1)} %copy.49), channel_id=1, source_target_pairs={{120,0},{0,8},{8,16},{16,24},{24,32},{32,40},{40,48},{48,56},{56,6... | collective-permute-start | bytes 147464 | tf_op jit(solution)/shard_map/while/body/eval_jaxpr/ppermute | solution.py:15
  492.5 13.4 %collective-permute-start.1 = (bf16[192,1,128]{2,0,1:T(8,128)(2,1)S(1)}, bf16[192,1,128]{2,0,1:T(8,128)(2,1)S(1)}, u32[]{:S(2)}, u32[]{:S(2)}) collective-permute-start(bf16[192,1,128]{2,0,1:T(8,128)(2,1)S(1)} %copy.50), channel_id=1, source_target_pairs={{120,0},{0,8},{8,16},{16,24},{24,32},{32,40},{40,48},{48,56},{56,6... | collective-permute-start | bytes 147464 | tf_op jit(solution)/shard_map/while/body/eval_jaxpr/ppermute | solution.py:15
  497.5 12.5 %collective-permute-start.3 = (f32[192,1,128]{2,0,1:T(8,128)S(1)}, f32[192,1,128]{2,0,1:T(8,128)S(1)}, u32[]{:S(2)}, u32[]{:S(2)}) collective-permute-start(f32[192,1,128]{2,0,1:T(8,128)S(1)} %fusion.107), channel_id=1, source_target_pairs={{120,0},{0,8},{8,16},{16,24},{24,32},{32,40},{40,48},{48,56},{56,6... | collective-permute-start | bytes 294920 | tf_op jit(solution)/shard_map/while/body/eval_jaxpr/ppermute | solution.py:15
  499.7 12.5 %collective-permute-start.4 = (f32[192,1,128]{2,0,1:T(8,128)S(1)}, f32[192,1,128]{2,0,1:T(8,128)S(1)}, u32[]{:S(2)}, u32[]{:S(2)}) collective-permute-start(f32[192,1,128]{2,0,1:T(8,128)S(1)} %fusion.108), channel_id=1, source_target_pairs={{120,0},{0,8},{8,16},{16,24},{24,32},{32,40},{40,48},{48,56},{56,6... | collective-permute-start | bytes 294920 | tf_op jit(solution)/shard_map/while/body/eval_jaxpr/ppermute | solution.py:15
  512.2 15.3 %collective-permute-start = (bf16[192,1,128]{2,0,1:T(8,128)(2,1)S(1)}, bf16[192,1,128]{2,0,1:T(8,128)(2,1)S(1)}, u32[]{:S(2)}, u32[]{:S(2)}) collective-permute-start(bf16[192,1,128]{2,0,1:T(8,128)(2,1)S(1)} %copy.49), channel_id=1, source_target_pairs={{120,0},{0,8},{8,16},{16,24},{24,32},{32,40},{40,48},{48,56},{56,6... | collective-permute-start | bytes 147464 | tf_op jit(solution)/shard_map/while/body/eval_jaxpr/ppermute | solution.py:15
  514.2 13.4 %collective-permute-start.1 = (bf16[192,1,128]{2,0,1:T(8,128)(2,1)S(1)}, bf16[192,1,128]{2,0,1:T(8,128)(2,1)S(1)}, u32[]{:S(2)}, u32[]{:S(2)}) collective-permute-start(bf16[192,1,128]{2,0,1:T(8,128)(2,1)S(1)} %copy.50), channel_id=1, source_target_pairs={{120,0},{0,8},{8,16},{16,24},{24,32},{32,40},{40,48},{48,56},{56,6... | collective-permute-start | bytes 147464 | tf_op jit(solution)/shard_map/while/body/eval_jaxpr/ppermute | solution.py:15
  519.1 12.5 %collective-permute-start.3 = (f32[192,1,128]{2,0,1:T(8,128)S(1)}, f32[192,1,128]{2,0,1:T(8,128)S(1)}, u32[]{:S(2)}, u32[]{:S(2)}) collective-permute-start(f32[192,1,128]{2,0,1:T(8,128)S(1)} %fusion.107), channel_id=1, source_target_pairs={{120,0},{0,8},{8,16},{16,24},{24,32},{32,40},{40,48},{48,56},{56,6... | collective-permute-start | bytes 294920 | tf_op jit(solution)/shard_map/while/body/eval_jaxpr/ppermute | solution.py:15
  521.3 12.5 %collective-permute-start.4 = (f32[192,1,128]{2,0,1:T(8,128)S(1)}, f32[192,1,128]{2,0,1:T(8,128)S(1)}, u32[]{:S(2)}, u32[]{:S(2)}) collective-permute-start(f32[192,1,128]{2,0,1:T(8,128)S(1)} %fusion.108), channel_id=1, source_target_pairs={{120,0},{0,8},{8,16},{16,24},{24,32},{32,40},{40,48},{48,56},{56,6... | collective-permute-start | bytes 294920 | tf_op jit(solution)/shard_map/while/body/eval_jaxpr/ppermute | solution.py:15
  533.8 15.3 %collective-permute-start = (bf16[192,1,128]{2,0,1:T(8,128)(2,1)S(1)}, bf16[192,1,128]{2,0,1:T(8,128)(2,1)S(1)}, u32[]{:S(2)}, u32[]{:S(2)}) collective-permute-start(bf16[192,1,128]{2,0,1:T(8,128)(2,1)S(1)} %copy.49), channel_id=1, source_target_pairs={{120,0},{0,8},{8,16},{16,24},{24,32},{32,40},{40,48},{48,56},{56,6... | collective-permute-start | bytes 147464 | tf_op jit(solution)/shard_map/while/body/eval_jaxpr/ppermute | solution.py:15
  535.8 13.4 %collective-permute-start.1 = (bf16[192,1,128]{2,0,1:T(8,128)(2,1)S(1)}, bf16[192,1,128]{2,0,1:T(8,128)(2,1)S(1)}, u32[]{:S(2)}, u32[]{:S(2)}) collective-permute-start(bf16[192,1,128]{2,0,1:T(8,128)(2,1)S(1)} %copy.50), channel_id=1, source_target_pairs={{120,0},{0,8},{8,16},{16,24},{24,32},{32,40},{40,48},{48,56},{56,6... | collective-permute-start | bytes 147464 | tf_op jit(solution)/shard_map/while/body/eval_jaxpr/ppermute | solution.py:15
  540.7 12.5 %collective-permute-start.3 = (f32[192,1,128]{2,0,1:T(8,128)S(1)}, f32[192,1,128]{2,0,1:T(8,128)S(1)}, u32[]{:S(2)}, u32[]{:S(2)}) collective-permute-start(f32[192,1,128]{2,0,1:T(8,128)S(1)} %fusion.107), channel_id=1, source_target_pairs={{120,0},{0,8},{8,16},{16,24},{24,32},{32,40},{40,48},{48,56},{56,6... | collective-permute-start | bytes 294920 | tf_op jit(solution)/shard_map/while/body/eval_jaxpr/ppermute | solution.py:15
  542.9 12.5 %collective-permute-start.4 = (f32[192,1,128]{2,0,1:T(8,128)S(1)}, f32[192,1,128]{2,0,1:T(8,128)S(1)}, u32[]{:S(2)}, u32[]{:S(2)}) collective-permute-start(f32[192,1,128]{2,0,1:T(8,128)S(1)} %fusion.108), channel_id=1, source_target_pairs={{120,0},{0,8},{8,16},{16,24},{24,32},{32,40},{40,48},{48,56},{56,6... | collective-permute-start | bytes 294920 | tf_op jit(solution)/shard_map/while/body/eval_jaxpr/ppermute | solution.py:15
  555.5 15.3 %collective-permute-start = (bf16[192,1,128]{2,0,1:T(8,128)(2,1)S(1)}, bf16[192,1,128]{2,0,1:T(8,128)(2,1)S(1)}, u32[]{:S(2)}, u32[]{:S(2)}) collective-permute-start(bf16[192,1,128]{2,0,1:T(8,128)(2,1)S(1)} %copy.49), channel_id=1, source_target_pairs={{120,0},{0,8},{8,16},{16,24},{24,32},{32,40},{40,48},{48,56},{56,6... | collective-permute-start | bytes 147464 | tf_op jit(solution)/shard_map/while/body/eval_jaxpr/ppermute | solution.py:15
  557.4 13.4 %collective-permute-start.1 = (bf16[192,1,128]{2,0,1:T(8,128)(2,1)S(1)}, bf16[192,1,128]{2,0,1:T(8,128)(2,1)S(1)}, u32[]{:S(2)}, u32[]{:S(2)}) collective-permute-start(bf16[192,1,128]{2,0,1:T(8,128)(2,1)S(1)} %copy.50), channel_id=1, source_target_pairs={{120,0},{0,8},{8,16},{16,24},{24,32},{32,40},{40,48},{48,56},{56,6... | collective-permute-start | bytes 147464 | tf_op jit(solution)/shard_map/while/body/eval_jaxpr/ppermute | solution.py:15
  562.3 12.5 %collective-permute-start.3 = (f32[192,1,128]{2,0,1:T(8,128)S(1)}, f32[192,1,128]{2,0,1:T(8,128)S(1)}, u32[]{:S(2)}, u32[]{:S(2)}) collective-permute-start(f32[192,1,128]{2,0,1:T(8,128)S(1)} %fusion.107), channel_id=1, source_target_pairs={{120,0},{0,8},{8,16},{16,24},{24,32},{32,40},{40,48},{48,56},{56,6... | collective-permute-start | bytes 294920 | tf_op jit(solution)/shard_map/while/body/eval_jaxpr/ppermute | solution.py:15
  564.5 12.5 %collective-permute-start.4 = (f32[192,1,128]{2,0,1:T(8,128)S(1)}, f32[192,1,128]{2,0,1:T(8,128)S(1)}, u32[]{:S(2)}, u32[]{:S(2)}) collective-permute-start(f32[192,1,128]{2,0,1:T(8,128)S(1)} %fusion.108), channel_id=1, source_target_pairs={{120,0},{0,8},{8,16},{16,24},{24,32},{32,40},{40,48},{48,56},{56,6... | collective-permute-start | bytes 294920 | tf_op jit(solution)/shard_map/while/body/eval_jaxpr/ppermute | solution.py:15
  577.1 15.3 %collective-permute-start = (bf16[192,1,128]{2,0,1:T(8,128)(2,1)S(1)}, bf16[192,1,128]{2,0,1:T(8,128)(2,1)S(1)}, u32[]{:S(2)}, u32[]{:S(2)}) collective-permute-start(bf16[192,1,128]{2,0,1:T(8,128)(2,1)S(1)} %copy.49), channel_id=1, source_target_pairs={{120,0},{0,8},{8,16},{16,24},{24,32},{32,40},{40,48},{48,56},{56,6... | collective-permute-start | bytes 147464 | tf_op jit(solution)/shard_map/while/body/eval_jaxpr/ppermute | solution.py:15
  579.0 13.4 %collective-permute-start.1 = (bf16[192,1,128]{2,0,1:T(8,128)(2,1)S(1)}, bf16[192,1,128]{2,0,1:T(8,128)(2,1)S(1)}, u32[]{:S(2)}, u32[]{:S(2)}) collective-permute-start(bf16[192,1,128]{2,0,1:T(8,128)(2,1)S(1)} %copy.50), channel_id=1, source_target_pairs={{120,0},{0,8},{8,16},{16,24},{24,32},{32,40},{40,48},{48,56},{56,6... | collective-permute-start | bytes 147464 | tf_op jit(solution)/shard_map/while/body/eval_jaxpr/ppermute | solution.py:15
  583.9 12.5 %collective-permute-start.3 = (f32[192,1,128]{2,0,1:T(8,128)S(1)}, f32[192,1,128]{2,0,1:T(8,128)S(1)}, u32[]{:S(2)}, u32[]{:S(2)}) collective-permute-start(f32[192,1,128]{2,0,1:T(8,128)S(1)} %fusion.107), channel_id=1, source_target_pairs={{120,0},{0,8},{8,16},{16,24},{24,32},{32,40},{40,48},{48,56},{56,6... | collective-permute-start | bytes 294920 | tf_op jit(solution)/shard_map/while/body/eval_jaxpr/ppermute | solution.py:15
  586.1 12.5 %collective-permute-start.4 = (f32[192,1,128]{2,0,1:T(8,128)S(1)}, f32[192,1,128]{2,0,1:T(8,128)S(1)}, u32[]{:S(2)}, u32[]{:S(2)}) collective-permute-start(f32[192,1,128]{2,0,1:T(8,128)S(1)} %fusion.108), channel_id=1, source_target_pairs={{120,0},{0,8},{8,16},{16,24},{24,32},{32,40},{40,48},{48,56},{56,6... | collective-permute-start | bytes 294920 | tf_op jit(solution)/shard_map/while/body/eval_jaxpr/ppermute | solution.py:15
  598.7 15.3 %collective-permute-start = (bf16[192,1,128]{2,0,1:T(8,128)(2,1)S(1)}, bf16[192,1,128]{2,0,1:T(8,128)(2,1)S(1)}, u32[]{:S(2)}, u32[]{:S(2)}) collective-permute-start(bf16[192,1,128]{2,0,1:T(8,128)(2,1)S(1)} %copy.49), channel_id=1, source_target_pairs={{120,0},{0,8},{8,16},{16,24},{24,32},{32,40},{40,48},{48,56},{56,6... | collective-permute-start | bytes 147464 | tf_op jit(solution)/shard_map/while/body/eval_jaxpr/ppermute | solution.py:15
  600.6 13.4 %collective-permute-start.1 = (bf16[192,1,128]{2,0,1:T(8,128)(2,1)S(1)}, bf16[192,1,128]{2,0,1:T(8,128)(2,1)S(1)}, u32[]{:S(2)}, u32[]{:S(2)}) collective-permute-start(bf16[192,1,128]{2,0,1:T(8,128)(2,1)S(1)} %copy.50), channel_id=1, source_target_pairs={{120,0},{0,8},{8,16},{16,24},{24,32},{32,40},{40,48},{48,56},{56,6... | collective-permute-start | bytes 147464 | tf_op jit(solution)/shard_map/while/body/eval_jaxpr/ppermute | solution.py:15
  605.5 12.5 %collective-permute-start.3 = (f32[192,1,128]{2,0,1:T(8,128)S(1)}, f32[192,1,128]{2,0,1:T(8,128)S(1)}, u32[]{:S(2)}, u32[]{:S(2)}) collective-permute-start(f32[192,1,128]{2,0,1:T(8,128)S(1)} %fusion.107), channel_id=1, source_target_pairs={{120,0},{0,8},{8,16},{16,24},{24,32},{32,40},{40,48},{48,56},{56,6... | collective-permute-start | bytes 294920 | tf_op jit(solution)/shard_map/while/body/eval_jaxpr/ppermute | solution.py:15
  620.3 15.3 %collective-permute-start = (bf16[192,1,128]{2,0,1:T(8,128)(2,1)S(1)}, bf16[192,1,128]{2,0,1:T(8,128)(2,1)S(1)}, u32[]{:S(2)}, u32[]{:S(2)}) collective-permute-start(bf16[192,1,128]{2,0,1:T(8,128)(2,1)S(1)} %copy.49), channel_id=1, source_target_pairs={{120,0},{0,8},{8,16},{16,24},{24,32},{32,40},{40,48},{48,56},{56,6... | collective-permute-start | bytes 147464 | tf_op jit(solution)/shard_map/while/body/eval_jaxpr/ppermute | solution.py:15
  622.2 13.4 %collective-permute-start.1 = (bf16[192,1,128]{2,0,1:T(8,128)(2,1)S(1)}, bf16[192,1,128]{2,0,1:T(8,128)(2,1)S(1)}, u32[]{:S(2)}, u32[]{:S(2)}) collective-permute-start(bf16[192,1,128]{2,0,1:T(8,128)(2,1)S(1)} %copy.50), channel_id=1, source_target_pairs={{120,0},{0,8},{8,16},{16,24},{24,32},{32,40},{40,48},{48,56},{56,6... | collective-permute-start | bytes 147464 | tf_op jit(solution)/shard_map/while/body/eval_jaxpr/ppermute | solution.py:15
  (21 other events, 389.7 us)
Sparse Core Ops, SparseCore 0:
  10.2 123.6 all-gather.5
  136.0 114.9 all-gather.7
  650.4 439.0 reduce-scatter.3
where the time goes:
time: 1100 us
  waiting for transfers between devices  742 us (67%)
  starting transfers between devices  154 us (14%)
  blocking collectives  123 us (11%)
  matrix products  40.3 us (4%)
  between operations  14.5 us (1%)
  local copies, waits for them, and re-layouts  12.7 us (1%)
    unnamed x4, waiting for transfers between devices  440 us
    ppermute x80, waiting for transfers between devices, passed_along(): return lax.ppermute(block, axis, route)  163 us
    ppermute x80, starting transfers between devices, passed_along(): return lax.ppermute(block, axis, route)  154 us
    all_gather x1, waiting for transfers between devices, body(): lax.all_gather(value_proj, ('dp', 'context'), axis=0, tiled=True)  76.3 us
    all_gather x1, waiting for transfers between devices, body(): lax.all_gather(key_proj, ('dp', 'context'), axis=0, tiled=True)  62.4 us
    unnamed x1, blocking collectives  56.4 us
    all_gather x1, blocking collectives, body(): lax.all_gather(values, 'context', axis=0, tiled=True)  33.5 us
    all_gather x1, blocking collectives, body(): lax.all_gather(keys, 'context', axis=0, tiled=True)  33.5 us
  transfers between devices with their start and end apart: 83, of which 51 were waited for; matrix products, arithmetic and copies ran while one was open for 4% of the time, Pallas kernels for 0%

commit v1 on v0

--- a/solution.py
+++ b/solution.py
@@ -7,6 +7,11 @@
 KV_HEADS = 8
 HEAD_DIM = 128
 far_below = -1e30
+
+
+def swapped_in(block, mesh_axis, dim):
+    repeated = jnp.stack([block] * lax.axis_size(mesh_axis))
+    return jnp.concatenate(lax.all_to_all(repeated, mesh_axis, 0, 0), axis=dim)
 
 
 def passed_along(block, axis, distance):
@@ -24,7 +29,7 @@
     steps = lax.axis_size("context")
     pieces = (
         lax.all_gather(key_proj, ("dp", "context"), axis=0, tiled=True),
-        lax.all_gather(value_proj, ("dp", "context"), axis=0, tiled=True),
+        swapped_in(value_proj, ("dp", "context"), 0),
     )
     columns = local_rows
     key_sum = jnp.dot(columns, pieces[0], preferred_element_type=jnp.float32)

time: 1100 us -> 1030 us (0.936)
  the two profiles are of different devices: /device:TPU:8 before, /device:TPU:16 now
where the time goes in v1:
time: 1030 us; the launch traced here: 1020 us
  waiting for transfers between devices  650 us (63%)
  starting transfers between devices  171 us (17%)
  blocking collectives  122 us (12%)
  matrix products  40.2 us (4%)
  local copies, waits for them, and re-layouts  18.2 us (2%)
  between operations  14.9 us (1%)
    unnamed x3, waiting for transfers between devices  439 us
    ppermute x80, waiting for transfers between devices, passed_along(): return lax.ppermute(block, axis, route)  163 us
    ppermute x80, starting transfers between devices, passed_along(): return lax.ppermute(block, axis, route)  155 us
    unnamed x1, blocking collectives  58.9 us
    all_gather x1, waiting for transfers between devices, body(): lax.all_gather(key_proj, ('dp', 'context'), axis=0, tiled=True)  47.9 us
    all_gather x1, blocking collectives, body(): lax.all_gather(keys, 'context', axis=0, tiled=True)  33.9 us
    all_gather x1, blocking collectives, body(): lax.all_gather(values, 'context', axis=0, tiled=True)  29.6 us
  transfers between devices with their start and end apart: 83, of which 50 were waited for; matrix products, arithmetic and copies ran while one was open for 4% of the time, Pallas kernels for 0%

profile of v1, /device:TPU:16, one launch (start us, length us, event | category | flops | bytes accessed | tf_op | source)
XLA Modules:
  0.0 1024.5 jit_solution(718537736535189762)
XLA Ops:
  9.9 16.3 %all-to-all-start = ((bf16[64,64,128]{2,1,0:T(8,128)(2,1)}), bf16[64,64,128]{2,1,0:T(8,128)(2,1)}, u32[]{:S(2)}, u32[]{:S(2)}) async-start(bf16[64,64,128]{2,1,0:T(8,128)(2,1)} %stack.2), calls=%async_computation | async-start | bytes 2097152 | tf_op jit(solution)/shard_map/all_to_all | solution.py:14
  32.1 58.9 %all-reduce = bf16[3072]{0:T(1024)(128)(2,1)S(1)} all-reduce(bf16[3072]{0:T(1024)(128)(2,1)S(1)} %dynamic-update-slice), channel_id=2, replica_groups=mesh['dp'=4,'context'=16,'head'=8] {'context'}, use_global_device_ids=true, to_apply=%add | all-reduce | flops 3072 | bytes 12288
  91.4 47.9 %all-gather.5.cloned.1.call-done = bf16[4096,128]{1,0:T(8,128)(2,1)} async-done(((bf16[64,128]{1,0:T(8,128)(2,1)}), bf16[4096,128]{1,0:T(8,128)(2,1)}) %all-gather.5.cloned.1.call-update) | async-done | bytes 1048592 | tf_op jit(solution)/shard_map/all_gather | solution.py:31
  141.1 33.9 %all-gather.1 = bf16[3072,128]{1,0:T(8,128)(2,1)S(1)} all-gather(bf16[192,128]{1,0:T(8,128)(2,1)S(1)} %fusion.40), channel_id=3, replica_groups=mesh['dp'=4,'context'=16,'head'=8] {'context'}, dimensions={0}, use_global_device_ids=true | all-gather | bytes 835584 | tf_op jit(solution)/shard_map/all_gather | solution.py:54
  175.0 2.0 fusion.25
  177.0 3.6 copy-done.1
  180.6 3.2 fusion.27
  185.7 29.6 %all-gather.2 = bf16[3072,128]{1,0:T(8,128)(2,1)S(1)} all-gather(bf16[192,128]{1,0:T(8,128)(2,1)S(1)} %fusion.43), channel_id=4, replica_groups=mesh['dp'=4,'context'=16,'head'=8] {'context'}, dimensions={0}, use_global_device_ids=true | all-gather | bytes 835584 | tf_op jit(solution)/shard_map/all_gather | solution.py:55
  215.2 6.2 fusion.61
  221.5 347.1 %while.21 = (s32[]{:T(128)}, bf16[192,1,128]{2,0,1:T(8,128)(2,1)S(1)}, bf16[192,1,128]{2,0,1:T(8,128)(2,1)S(1)}, bf16[192]{0:T(256)(128)(2,1)S(1)}, f32[192,1,12...) while((s32[]{:T(128)}, ...), condition=%wide.region_4.5_spmd.clone, body=%wide.region_3.4_spmd.clone.sunk | while | flops 190328832 | bytes 6227287 | solution.py:111
  221.5 2.3 collective-permute-start
  223.8 2.4 collective-permute-start.1
  226.2 2.3 collective-permute-start.2
  234.1 3.6 collective-permute-done.2
  237.7 4.4 collective-permute-done.3
  242.0 2.2 collective-permute-done.4
  255.7 3.9 collective-permute-done.2
  259.6 4.1 collective-permute-done.3
  263.7 2.2 collective-permute-done.4
  277.3 3.9 collective-permute-done.2
  281.2 4.1 collective-permute-done.3
  285.3 2.2 collective-permute-done.4
  298.9 3.9 collective-permute-done.2
  302.8 4.1 collective-permute-done.3
  306.9 2.2 collective-permute-done.4
  320.5 3.9 collective-permute-done.2
  324.5 4.1 collective-permute-done.3
  328.5 2.2 collective-permute-done.4
  342.2 3.9 collective-permute-done.2
  346.1 4.1 collective-permute-done.3
  350.1 2.2 collective-permute-done.4
  363.8 3.9 collective-permute-done.2
  367.7 4.1 collective-permute-done.3
  371.8 2.2 collective-permute-done.4
  385.4 3.9 collective-permute-done.2
  389.3 4.1 collective-permute-done.3
  393.4 2.2 collective-permute-done.4
  407.0 3.9 collective-permute-done.2
  410.9 4.1 collective-permute-done.3
  415.0 2.2 collective-permute-done.4
  428.6 3.9 collective-permute-done.2
  432.6 4.1 collective-permute-done.3
  436.6 2.2 collective-permute-done.4
  450.3 3.9 collective-permute-done.2
  454.2 4.1 collective-permute-done.3
  458.2 2.2 collective-permute-done.4
  471.9 3.9 collective-permute-done.2
  475.8 4.1 collective-permute-done.3
  479.9 2.2 collective-permute-done.4
  493.5 3.9 collective-permute-done.2
  497.4 4.1 collective-permute-done.3
  501.5 2.2 collective-permute-done.4
  515.1 3.9 collective-permute-done.2
  519.0 4.1 collective-permute-done.3
  523.1 2.2 collective-permute-done.4
  536.7 3.9 collective-permute-done.2
  540.7 4.1 collective-permute-done.3
  544.7 2.2 collective-permute-done.4
  558.4 3.9 collective-permute-done.2
  562.3 4.1 collective-permute-done.3
  566.3 2.2 collective-permute-done.4
  568.6 2.7 convolution_bitcast_fusion.3
  571.3 5.6 copy.31
  577.9 438.5 %reduce-scatter.4.cloned.1.call-done = f32[64,256]{1,0:T(8,128)} async-done(((f32[4096,256]{1,0:T(8,128)}), f32[64,256]{1,0:T(8,128)}) %reduce-scatter.4.cloned.1.call-update) | async-done | bytes 65552
  (285 shorter events, 189.5 us)
Async XLA Ops:
  7.2 132.1 %all-gather.5.cloned.1.call-start = ((), (), s32[]{:S(2)}) async-start(), calls=%async_computation.2 | async-start | bytes 1064960 | tf_op jit(solution)/shard_map/all_gather | solution.py:31
  9.9 174.0 %all-to-all-start = ((bf16[64,64,128]{2,1,0:T(8,128)(2,1)}), bf16[64,64,128]{2,1,0:T(8,128)(2,1)}, u32[]{:S(2)}, u32[]{:S(2)}) async-start(bf16[64,64,128]{2,1,0:T(8,128)(2,1)} %stack.2), calls=%async_computation | async-start | bytes 2097152 | tf_op jit(solution)/shard_map/all_to_all | solution.py:14
  26.1 990.2 %reduce-scatter.4.cloned.1.call-start = ((), (), s32[]{:S(2)}) async-start(), calls=%async_computation.3 | async-start | bytes 4259840
  221.5 16.2 %collective-permute-start = (bf16[192,1,128]{2,0,1:T(8,128)(2,1)S(1)}, bf16[192,1,128]{2,0,1:T(8,128)(2,1)S(1)}, u32[]{:S(2)}, u32[]{:S(2)}) collective-permute-start(bf16[192,1,128]{2,0,1:T(8,128)(2,1)S(1)} %copy.49), channel_id=1, source_target_pairs={{120,0},{0,8},{8,16},{16,24},{24,32},{32,40},{40,48},{48,56},{56,6... | collective-permute-start | bytes 147464 | tf_op jit(solution)/shard_map/while/body/eval_jaxpr/ppermute | solution.py:20
  223.8 13.9 %collective-permute-start.1 = (bf16[192,1,128]{2,0,1:T(8,128)(2,1)S(1)}, bf16[192,1,128]{2,0,1:T(8,128)(2,1)S(1)}, u32[]{:S(2)}, u32[]{:S(2)}) collective-permute-start(bf16[192,1,128]{2,0,1:T(8,128)(2,1)S(1)} %copy.50), channel_id=1, source_target_pairs={{120,0},{0,8},{8,16},{16,24},{24,32},{32,40},{40,48},{48,56},{56,6... | collective-permute-start | bytes 147464 | tf_op jit(solution)/shard_map/while/body/eval_jaxpr/ppermute | solution.py:20
  229.5 12.5 %collective-permute-start.3 = (f32[192,1,128]{2,0,1:T(8,128)S(1)}, f32[192,1,128]{2,0,1:T(8,128)S(1)}, u32[]{:S(2)}, u32[]{:S(2)}) collective-permute-start(f32[192,1,128]{2,0,1:T(8,128)S(1)} %fusion.107), channel_id=1, source_target_pairs={{120,0},{0,8},{8,16},{16,24},{24,32},{32,40},{40,48},{48,56},{56,6... | collective-permute-start | bytes 294920 | tf_op jit(solution)/shard_map/while/body/eval_jaxpr/ppermute | solution.py:20
  231.7 12.5 %collective-permute-start.4 = (f32[192,1,128]{2,0,1:T(8,128)S(1)}, f32[192,1,128]{2,0,1:T(8,128)S(1)}, u32[]{:S(2)}, u32[]{:S(2)}) collective-permute-start(f32[192,1,128]{2,0,1:T(8,128)S(1)} %fusion.108), channel_id=1, source_target_pairs={{120,0},{0,8},{8,16},{16,24},{24,32},{32,40},{40,48},{48,56},{56,6... | collective-permute-start | bytes 294920 | tf_op jit(solution)/shard_map/while/body/eval_jaxpr/ppermute | solution.py:20
  244.3 15.3 %collective-permute-start = (bf16[192,1,128]{2,0,1:T(8,128)(2,1)S(1)}, bf16[192,1,128]{2,0,1:T(8,128)(2,1)S(1)}, u32[]{:S(2)}, u32[]{:S(2)}) collective-permute-start(bf16[192,1,128]{2,0,1:T(8,128)(2,1)S(1)} %copy.49), channel_id=1, source_target_pairs={{120,0},{0,8},{8,16},{16,24},{24,32},{32,40},{40,48},{48,56},{56,6... | collective-permute-start | bytes 147464 | tf_op jit(solution)/shard_map/while/body/eval_jaxpr/ppermute | solution.py:20
  246.2 13.4 %collective-permute-start.1 = (bf16[192,1,128]{2,0,1:T(8,128)(2,1)S(1)}, bf16[192,1,128]{2,0,1:T(8,128)(2,1)S(1)}, u32[]{:S(2)}, u32[]{:S(2)}) collective-permute-start(bf16[192,1,128]{2,0,1:T(8,128)(2,1)S(1)} %copy.50), channel_id=1, source_target_pairs={{120,0},{0,8},{8,16},{16,24},{24,32},{32,40},{40,48},{48,56},{56,6... | collective-permute-start | bytes 147464 | tf_op jit(solution)/shard_map/while/body/eval_jaxpr/ppermute | solution.py:20
  251.1 12.5 %collective-permute-start.3 = (f32[192,1,128]{2,0,1:T(8,128)S(1)}, f32[192,1,128]{2,0,1:T(8,128)S(1)}, u32[]{:S(2)}, u32[]{:S(2)}) collective-permute-start(f32[192,1,128]{2,0,1:T(8,128)S(1)} %fusion.107), channel_id=1, source_target_pairs={{120,0},{0,8},{8,16},{16,24},{24,32},{32,40},{40,48},{48,56},{56,6... | collective-permute-start | bytes 294920 | tf_op jit(solution)/shard_map/while/body/eval_jaxpr/ppermute | solution.py:20
  253.3 12.5 %collective-permute-start.4 = (f32[192,1,128]{2,0,1:T(8,128)S(1)}, f32[192,1,128]{2,0,1:T(8,128)S(1)}, u32[]{:S(2)}, u32[]{:S(2)}) collective-permute-start(f32[192,1,128]{2,0,1:T(8,128)S(1)} %fusion.108), channel_id=1, source_target_pairs={{120,0},{0,8},{8,16},{16,24},{24,32},{32,40},{40,48},{48,56},{56,6... | collective-permute-start | bytes 294920 | tf_op jit(solution)/shard_map/while/body/eval_jaxpr/ppermute | solution.py:20
  265.9 15.3 %collective-permute-start = (bf16[192,1,128]{2,0,1:T(8,128)(2,1)S(1)}, bf16[192,1,128]{2,0,1:T(8,128)(2,1)S(1)}, u32[]{:S(2)}, u32[]{:S(2)}) collective-permute-start(bf16[192,1,128]{2,0,1:T(8,128)(2,1)S(1)} %copy.49), channel_id=1, source_target_pairs={{120,0},{0,8},{8,16},{16,24},{24,32},{32,40},{40,48},{48,56},{56,6... | collective-permute-start | bytes 147464 | tf_op jit(solution)/shard_map/while/body/eval_jaxpr/ppermute | solution.py:20
  267.8 13.4 %collective-permute-start.1 = (bf16[192,1,128]{2,0,1:T(8,128)(2,1)S(1)}, bf16[192,1,128]{2,0,1:T(8,128)(2,1)S(1)}, u32[]{:S(2)}, u32[]{:S(2)}) collective-permute-start(bf16[192,1,128]{2,0,1:T(8,128)(2,1)S(1)} %copy.50), channel_id=1, source_target_pairs={{120,0},{0,8},{8,16},{16,24},{24,32},{32,40},{40,48},{48,56},{56,6... | collective-permute-start | bytes 147464 | tf_op jit(solution)/shard_map/while/body/eval_jaxpr/ppermute | solution.py:20
  272.7 12.5 %collective-permute-start.3 = (f32[192,1,128]{2,0,1:T(8,128)S(1)}, f32[192,1,128]{2,0,1:T(8,128)S(1)}, u32[]{:S(2)}, u32[]{:S(2)}) collective-permute-start(f32[192,1,128]{2,0,1:T(8,128)S(1)} %fusion.107), channel_id=1, source_target_pairs={{120,0},{0,8},{8,16},{16,24},{24,32},{32,40},{40,48},{48,56},{56,6... | collective-permute-start | bytes 294920 | tf_op jit(solution)/shard_map/while/body/eval_jaxpr/ppermute | solution.py:20
  275.0 12.5 %collective-permute-start.4 = (f32[192,1,128]{2,0,1:T(8,128)S(1)}, f32[192,1,128]{2,0,1:T(8,128)S(1)}, u32[]{:S(2)}, u32[]{:S(2)}) collective-permute-start(f32[192,1,128]{2,0,1:T(8,128)S(1)} %fusion.108), channel_id=1, source_target_pairs={{120,0},{0,8},{8,16},{16,24},{24,32},{32,40},{40,48},{48,56},{56,6... | collective-permute-start | bytes 294920 | tf_op jit(solution)/shard_map/while/body/eval_jaxpr/ppermute | solution.py:20
  287.5 15.3 %collective-permute-start = (bf16[192,1,128]{2,0,1:T(8,128)(2,1)S(1)}, bf16[192,1,128]{2,0,1:T(8,128)(2,1)S(1)}, u32[]{:S(2)}, u32[]{:S(2)}) collective-permute-start(bf16[192,1,128]{2,0,1:T(8,128)(2,1)S(1)} %copy.49), channel_id=1, source_target_pairs={{120,0},{0,8},{8,16},{16,24},{24,32},{32,40},{40,48},{48,56},{56,6... | collective-permute-start | bytes 147464 | tf_op jit(solution)/shard_map/while/body/eval_jaxpr/ppermute | solution.py:20
  289.4 13.4 %collective-permute-start.1 = (bf16[192,1,128]{2,0,1:T(8,128)(2,1)S(1)}, bf16[192,1,128]{2,0,1:T(8,128)(2,1)S(1)}, u32[]{:S(2)}, u32[]{:S(2)}) collective-permute-start(bf16[192,1,128]{2,0,1:T(8,128)(2,1)S(1)} %copy.50), channel_id=1, source_target_pairs={{120,0},{0,8},{8,16},{16,24},{24,32},{32,40},{40,48},{48,56},{56,6... | collective-permute-start | bytes 147464 | tf_op jit(solution)/shard_map/while/body/eval_jaxpr/ppermute | solution.py:20
  294.4 12.5 %collective-permute-start.3 = (f32[192,1,128]{2,0,1:T(8,128)S(1)}, f32[192,1,128]{2,0,1:T(8,128)S(1)}, u32[]{:S(2)}, u32[]{:S(2)}) collective-permute-start(f32[192,1,128]{2,0,1:T(8,128)S(1)} %fusion.107), channel_id=1, source_target_pairs={{120,0},{0,8},{8,16},{16,24},{24,32},{32,40},{40,48},{48,56},{56,6... | collective-permute-start | bytes 294920 | tf_op jit(solution)/shard_map/while/body/eval_jaxpr/ppermute | solution.py:20
  296.6 12.5 %collective-permute-start.4 = (f32[192,1,128]{2,0,1:T(8,128)S(1)}, f32[192,1,128]{2,0,1:T(8,128)S(1)}, u32[]{:S(2)}, u32[]{:S(2)}) collective-permute-start(f32[192,1,128]{2,0,1:T(8,128)S(1)} %fusion.108), channel_id=1, source_target_pairs={{120,0},{0,8},{8,16},{16,24},{24,32},{32,40},{40,48},{48,56},{56,6... | collective-permute-start | bytes 294920 | tf_op jit(solution)/shard_map/while/body/eval_jaxpr/ppermute | solution.py:20
  309.1 15.3 %collective-permute-start = (bf16[192,1,128]{2,0,1:T(8,128)(2,1)S(1)}, bf16[192,1,128]{2,0,1:T(8,128)(2,1)S(1)}, u32[]{:S(2)}, u32[]{:S(2)}) collective-permute-start(bf16[192,1,128]{2,0,1:T(8,128)(2,1)S(1)} %copy.49), channel_id=1, source_target_pairs={{120,0},{0,8},{8,16},{16,24},{24,32},{32,40},{40,48},{48,56},{56,6... | collective-permute-start | bytes 147464 | tf_op jit(solution)/shard_map/while/body/eval_jaxpr/ppermute | solution.py:20
  311.1 13.4 %collective-permute-start.1 = (bf16[192,1,128]{2,0,1:T(8,128)(2,1)S(1)}, bf16[192,1,128]{2,0,1:T(8,128)(2,1)S(1)}, u32[]{:S(2)}, u32[]{:S(2)}) collective-permute-start(bf16[192,1,128]{2,0,1:T(8,128)(2,1)S(1)} %copy.50), channel_id=1, source_target_pairs={{120,0},{0,8},{8,16},{16,24},{24,32},{32,40},{40,48},{48,56},{56,6... | collective-permute-start | bytes 147464 | tf_op jit(solution)/shard_map/while/body/eval_jaxpr/ppermute | solution.py:20
  316.0 12.5 %collective-permute-start.3 = (f32[192,1,128]{2,0,1:T(8,128)S(1)}, f32[192,1,128]{2,0,1:T(8,128)S(1)}, u32[]{:S(2)}, u32[]{:S(2)}) collective-permute-start(f32[192,1,128]{2,0,1:T(8,128)S(1)} %fusion.107), channel_id=1, source_target_pairs={{120,0},{0,8},{8,16},{16,24},{24,32},{32,40},{40,48},{48,56},{56,6... | collective-permute-start | bytes 294920 | tf_op jit(solution)/shard_map/while/body/eval_jaxpr/ppermute | solution.py:20
  318.2 12.5 %collective-permute-start.4 = (f32[192,1,128]{2,0,1:T(8,128)S(1)}, f32[192,1,128]{2,0,1:T(8,128)S(1)}, u32[]{:S(2)}, u32[]{:S(2)}) collective-permute-start(f32[192,1,128]{2,0,1:T(8,128)S(1)} %fusion.108), channel_id=1, source_target_pairs={{120,0},{0,8},{8,16},{16,24},{24,32},{32,40},{40,48},{48,56},{56,6... | collective-permute-start | bytes 294920 | tf_op jit(solution)/shard_map/while/body/eval_jaxpr/ppermute | solution.py:20
  330.7 15.3 %collective-permute-start = (bf16[192,1,128]{2,0,1:T(8,128)(2,1)S(1)}, bf16[192,1,128]{2,0,1:T(8,128)(2,1)S(1)}, u32[]{:S(2)}, u32[]{:S(2)}) collective-permute-start(bf16[192,1,128]{2,0,1:T(8,128)(2,1)S(1)} %copy.49), channel_id=1, source_target_pairs={{120,0},{0,8},{8,16},{16,24},{24,32},{32,40},{40,48},{48,56},{56,6... | collective-permute-start | bytes 147464 | tf_op jit(solution)/shard_map/while/body/eval_jaxpr/ppermute | solution.py:20
  332.7 13.4 %collective-permute-start.1 = (bf16[192,1,128]{2,0,1:T(8,128)(2,1)S(1)}, bf16[192,1,128]{2,0,1:T(8,128)(2,1)S(1)}, u32[]{:S(2)}, u32[]{:S(2)}) collective-permute-start(bf16[192,1,128]{2,0,1:T(8,128)(2,1)S(1)} %copy.50), channel_id=1, source_target_pairs={{120,0},{0,8},{8,16},{16,24},{24,32},{32,40},{40,48},{48,56},{56,6... | collective-permute-start | bytes 147464 | tf_op jit(solution)/shard_map/while/body/eval_jaxpr/ppermute | solution.py:20
  337.6 12.5 %collective-permute-start.3 = (f32[192,1,128]{2,0,1:T(8,128)S(1)}, f32[192,1,128]{2,0,1:T(8,128)S(1)}, u32[]{:S(2)}, u32[]{:S(2)}) collective-permute-start(f32[192,1,128]{2,0,1:T(8,128)S(1)} %fusion.107), channel_id=1, source_target_pairs={{120,0},{0,8},{8,16},{16,24},{24,32},{32,40},{40,48},{48,56},{56,6... | collective-permute-start | bytes 294920 | tf_op jit(solution)/shard_map/while/body/eval_jaxpr/ppermute | solution.py:20
  339.8 12.5 %collective-permute-start.4 = (f32[192,1,128]{2,0,1:T(8,128)S(1)}, f32[192,1,128]{2,0,1:T(8,128)S(1)}, u32[]{:S(2)}, u32[]{:S(2)}) collective-permute-start(f32[192,1,128]{2,0,1:T(8,128)S(1)} %fusion.108), channel_id=1, source_target_pairs={{120,0},{0,8},{8,16},{16,24},{24,32},{32,40},{40,48},{48,56},{56,6... | collective-permute-start | bytes 294920 | tf_op jit(solution)/shard_map/while/body/eval_jaxpr/ppermute | solution.py:20
  352.4 15.3 %collective-permute-start = (bf16[192,1,128]{2,0,1:T(8,128)(2,1)S(1)}, bf16[192,1,128]{2,0,1:T(8,128)(2,1)S(1)}, u32[]{:S(2)}, u32[]{:S(2)}) collective-permute-start(bf16[192,1,128]{2,0,1:T(8,128)(2,1)S(1)} %copy.49), channel_id=1, source_target_pairs={{120,0},{0,8},{8,16},{16,24},{24,32},{32,40},{40,48},{48,56},{56,6... | collective-permute-start | bytes 147464 | tf_op jit(solution)/shard_map/while/body/eval_jaxpr/ppermute | solution.py:20
  354.3 13.4 %collective-permute-start.1 = (bf16[192,1,128]{2,0,1:T(8,128)(2,1)S(1)}, bf16[192,1,128]{2,0,1:T(8,128)(2,1)S(1)}, u32[]{:S(2)}, u32[]{:S(2)}) collective-permute-start(bf16[192,1,128]{2,0,1:T(8,128)(2,1)S(1)} %copy.50), channel_id=1, source_target_pairs={{120,0},{0,8},{8,16},{16,24},{24,32},{32,40},{40,48},{48,56},{56,6... | collective-permute-start | bytes 147464 | tf_op jit(solution)/shard_map/while/body/eval_jaxpr/ppermute | solution.py:20
  359.2 12.5 %collective-permute-start.3 = (f32[192,1,128]{2,0,1:T(8,128)S(1)}, f32[192,1,128]{2,0,1:T(8,128)S(1)}, u32[]{:S(2)}, u32[]{:S(2)}) collective-permute-start(f32[192,1,128]{2,0,1:T(8,128)S(1)} %fusion.107), channel_id=1, source_target_pairs={{120,0},{0,8},{8,16},{16,24},{24,32},{32,40},{40,48},{48,56},{56,6... | collective-permute-start | bytes 294920 | tf_op jit(solution)/shard_map/while/body/eval_jaxpr/ppermute | solution.py:20
  361.4 12.5 %collective-permute-start.4 = (f32[192,1,128]{2,0,1:T(8,128)S(1)}, f32[192,1,128]{2,0,1:T(8,128)S(1)}, u32[]{:S(2)}, u32[]{:S(2)}) collective-permute-start(f32[192,1,128]{2,0,1:T(8,128)S(1)} %fusion.108), channel_id=1, source_target_pairs={{120,0},{0,8},{8,16},{16,24},{24,32},{32,40},{40,48},{48,56},{56,6... | collective-permute-start | bytes 294920 | tf_op jit(solution)/shard_map/while/body/eval_jaxpr/ppermute | solution.py:20
  374.0 15.3 %collective-permute-start = (bf16[192,1,128]{2,0,1:T(8,128)(2,1)S(1)}, bf16[192,1,128]{2,0,1:T(8,128)(2,1)S(1)}, u32[]{:S(2)}, u32[]{:S(2)}) collective-permute-start(bf16[192,1,128]{2,0,1:T(8,128)(2,1)S(1)} %copy.49), channel_id=1, source_target_pairs={{120,0},{0,8},{8,16},{16,24},{24,32},{32,40},{40,48},{48,56},{56,6... | collective-permute-start | bytes 147464 | tf_op jit(solution)/shard_map/while/body/eval_jaxpr/ppermute | solution.py:20
  375.9 13.4 %collective-permute-start.1 = (bf16[192,1,128]{2,0,1:T(8,128)(2,1)S(1)}, bf16[192,1,128]{2,0,1:T(8,128)(2,1)S(1)}, u32[]{:S(2)}, u32[]{:S(2)}) collective-permute-start(bf16[192,1,128]{2,0,1:T(8,128)(2,1)S(1)} %copy.50), channel_id=1, source_target_pairs={{120,0},{0,8},{8,16},{16,24},{24,32},{32,40},{40,48},{48,56},{56,6... | collective-permute-start | bytes 147464 | tf_op jit(solution)/shard_map/while/body/eval_jaxpr/ppermute | solution.py:20
  380.8 12.5 %collective-permute-start.3 = (f32[192,1,128]{2,0,1:T(8,128)S(1)}, f32[192,1,128]{2,0,1:T(8,128)S(1)}, u32[]{:S(2)}, u32[]{:S(2)}) collective-permute-start(f32[192,1,128]{2,0,1:T(8,128)S(1)} %fusion.107), channel_id=1, source_target_pairs={{120,0},{0,8},{8,16},{16,24},{24,32},{32,40},{40,48},{48,56},{56,6... | collective-permute-start | bytes 294920 | tf_op jit(solution)/shard_map/while/body/eval_jaxpr/ppermute | solution.py:20
  383.1 12.5 %collective-permute-start.4 = (f32[192,1,128]{2,0,1:T(8,128)S(1)}, f32[192,1,128]{2,0,1:T(8,128)S(1)}, u32[]{:S(2)}, u32[]{:S(2)}) collective-permute-start(f32[192,1,128]{2,0,1:T(8,128)S(1)} %fusion.108), channel_id=1, source_target_pairs={{120,0},{0,8},{8,16},{16,24},{24,32},{32,40},{40,48},{48,56},{56,6... | collective-permute-start | bytes 294920 | tf_op jit(solution)/shard_map/while/body/eval_jaxpr/ppermute | solution.py:20
  395.6 15.3 %collective-permute-start = (bf16[192,1,128]{2,0,1:T(8,128)(2,1)S(1)}, bf16[192,1,128]{2,0,1:T(8,128)(2,1)S(1)}, u32[]{:S(2)}, u32[]{:S(2)}) collective-permute-start(bf16[192,1,128]{2,0,1:T(8,128)(2,1)S(1)} %copy.49), channel_id=1, source_target_pairs={{120,0},{0,8},{8,16},{16,24},{24,32},{32,40},{40,48},{48,56},{56,6... | collective-permute-start | bytes 147464 | tf_op jit(solution)/shard_map/while/body/eval_jaxpr/ppermute | solution.py:20
  397.5 13.4 %collective-permute-start.1 = (bf16[192,1,128]{2,0,1:T(8,128)(2,1)S(1)}, bf16[192,1,128]{2,0,1:T(8,128)(2,1)S(1)}, u32[]{:S(2)}, u32[]{:S(2)}) collective-permute-start(bf16[192,1,128]{2,0,1:T(8,128)(2,1)S(1)} %copy.50), channel_id=1, source_target_pairs={{120,0},{0,8},{8,16},{16,24},{24,32},{32,40},{40,48},{48,56},{56,6... | collective-permute-start | bytes 147464 | tf_op jit(solution)/shard_map/while/body/eval_jaxpr/ppermute | solution.py:20
  402.5 12.5 %collective-permute-start.3 = (f32[192,1,128]{2,0,1:T(8,128)S(1)}, f32[192,1,128]{2,0,1:T(8,128)S(1)}, u32[]{:S(2)}, u32[]{:S(2)}) collective-permute-start(f32[192,1,128]{2,0,1:T(8,128)S(1)} %fusion.107), channel_id=1, source_target_pairs={{120,0},{0,8},{8,16},{16,24},{24,32},{32,40},{40,48},{48,56},{56,6... | collective-permute-start | bytes 294920 | tf_op jit(solution)/shard_map/while/body/eval_jaxpr/ppermute | solution.py:20
  404.7 12.5 %collective-permute-start.4 = (f32[192,1,128]{2,0,1:T(8,128)S(1)}, f32[192,1,128]{2,0,1:T(8,128)S(1)}, u32[]{:S(2)}, u32[]{:S(2)}) collective-permute-start(f32[192,1,128]{2,0,1:T(8,128)S(1)} %fusion.108), channel_id=1, source_target_pairs={{120,0},{0,8},{8,16},{16,24},{24,32},{32,40},{40,48},{48,56},{56,6... | collective-permute-start | bytes 294920 | tf_op jit(solution)/shard_map/while/body/eval_jaxpr/ppermute | solution.py:20
  417.2 15.3 %collective-permute-start = (bf16[192,1,128]{2,0,1:T(8,128)(2,1)S(1)}, bf16[192,1,128]{2,0,1:T(8,128)(2,1)S(1)}, u32[]{:S(2)}, u32[]{:S(2)}) collective-permute-start(bf16[192,1,128]{2,0,1:T(8,128)(2,1)S(1)} %copy.49), channel_id=1, source_target_pairs={{120,0},{0,8},{8,16},{16,24},{24,32},{32,40},{40,48},{48,56},{56,6... | collective-permute-start | bytes 147464 | tf_op jit(solution)/shard_map/while/body/eval_jaxpr/ppermute | solution.py:20
  419.2 13.4 %collective-permute-start.1 = (bf16[192,1,128]{2,0,1:T(8,128)(2,1)S(1)}, bf16[192,1,128]{2,0,1:T(8,128)(2,1)S(1)}, u32[]{:S(2)}, u32[]{:S(2)}) collective-permute-start(bf16[192,1,128]{2,0,1:T(8,128)(2,1)S(1)} %copy.50), channel_id=1, source_target_pairs={{120,0},{0,8},{8,16},{16,24},{24,32},{32,40},{40,48},{48,56},{56,6... | collective-permute-start | bytes 147464 | tf_op jit(solution)/shard_map/while/body/eval_jaxpr/ppermute | solution.py:20
  424.1 12.5 %collective-permute-start.3 = (f32[192,1,128]{2,0,1:T(8,128)S(1)}, f32[192,1,128]{2,0,1:T(8,128)S(1)}, u32[]{:S(2)}, u32[]{:S(2)}) collective-permute-start(f32[192,1,128]{2,0,1:T(8,128)S(1)} %fusion.107), channel_id=1, source_target_pairs={{120,0},{0,8},{8,16},{16,24},{24,32},{32,40},{40,48},{48,56},{56,6... | collective-permute-start | bytes 294920 | tf_op jit(solution)/shard_map/while/body/eval_jaxpr/ppermute | solution.py:20
  426.3 12.5 %collective-permute-start.4 = (f32[192,1,128]{2,0,1:T(8,128)S(1)}, f32[192,1,128]{2,0,1:T(8,128)S(1)}, u32[]{:S(2)}, u32[]{:S(2)}) collective-permute-start(f32[192,1,128]{2,0,1:T(8,128)S(1)} %fusion.108), channel_id=1, source_target_pairs={{120,0},{0,8},{8,16},{16,24},{24,32},{32,40},{40,48},{48,56},{56,6... | collective-permute-start | bytes 294920 | tf_op jit(solution)/shard_map/while/body/eval_jaxpr/ppermute | solution.py:20
  438.8 15.3 %collective-permute-start = (bf16[192,1,128]{2,0,1:T(8,128)(2,1)S(1)}, bf16[192,1,128]{2,0,1:T(8,128)(2,1)S(1)}, u32[]{:S(2)}, u32[]{:S(2)}) collective-permute-start(bf16[192,1,128]{2,0,1:T(8,128)(2,1)S(1)} %copy.49), channel_id=1, source_target_pairs={{120,0},{0,8},{8,16},{16,24},{24,32},{32,40},{40,48},{48,56},{56,6... | collective-permute-start | bytes 147464 | tf_op jit(solution)/shard_map/while/body/eval_jaxpr/ppermute | solution.py:20
  440.8 13.4 %collective-permute-start.1 = (bf16[192,1,128]{2,0,1:T(8,128)(2,1)S(1)}, bf16[192,1,128]{2,0,1:T(8,128)(2,1)S(1)}, u32[]{:S(2)}, u32[]{:S(2)}) collective-permute-start(bf16[192,1,128]{2,0,1:T(8,128)(2,1)S(1)} %copy.50), channel_id=1, source_target_pairs={{120,0},{0,8},{8,16},{16,24},{24,32},{32,40},{40,48},{48,56},{56,6... | collective-permute-start | bytes 147464 | tf_op jit(solution)/shard_map/while/body/eval_jaxpr/ppermute | solution.py:20
  445.7 12.5 %collective-permute-start.3 = (f32[192,1,128]{2,0,1:T(8,128)S(1)}, f32[192,1,128]{2,0,1:T(8,128)S(1)}, u32[]{:S(2)}, u32[]{:S(2)}) collective-permute-start(f32[192,1,128]{2,0,1:T(8,128)S(1)} %fusion.107), channel_id=1, source_target_pairs={{120,0},{0,8},{8,16},{16,24},{24,32},{32,40},{40,48},{48,56},{56,6... | collective-permute-start | bytes 294920 | tf_op jit(solution)/shard_map/while/body/eval_jaxpr/ppermute | solution.py:20
  447.9 12.5 %collective-permute-start.4 = (f32[192,1,128]{2,0,1:T(8,128)S(1)}, f32[192,1,128]{2,0,1:T(8,128)S(1)}, u32[]{:S(2)}, u32[]{:S(2)}) collective-permute-start(f32[192,1,128]{2,0,1:T(8,128)S(1)} %fusion.108), channel_id=1, source_target_pairs={{120,0},{0,8},{8,16},{16,24},{24,32},{32,40},{40,48},{48,56},{56,6... | collective-permute-start | bytes 294920 | tf_op jit(solution)/shard_map/while/body/eval_jaxpr/ppermute | solution.py:20
  460.5 15.3 %collective-permute-start = (bf16[192,1,128]{2,0,1:T(8,128)(2,1)S(1)}, bf16[192,1,128]{2,0,1:T(8,128)(2,1)S(1)}, u32[]{:S(2)}, u32[]{:S(2)}) collective-permute-start(bf16[192,1,128]{2,0,1:T(8,128)(2,1)S(1)} %copy.49), channel_id=1, source_target_pairs={{120,0},{0,8},{8,16},{16,24},{24,32},{32,40},{40,48},{48,56},{56,6... | collective-permute-start | bytes 147464 | tf_op jit(solution)/shard_map/while/body/eval_jaxpr/ppermute | solution.py:20
  462.4 13.4 %collective-permute-start.1 = (bf16[192,1,128]{2,0,1:T(8,128)(2,1)S(1)}, bf16[192,1,128]{2,0,1:T(8,128)(2,1)S(1)}, u32[]{:S(2)}, u32[]{:S(2)}) collective-permute-start(bf16[192,1,128]{2,0,1:T(8,128)(2,1)S(1)} %copy.50), channel_id=1, source_target_pairs={{120,0},{0,8},{8,16},{16,24},{24,32},{32,40},{40,48},{48,56},{56,6... | collective-permute-start | bytes 147464 | tf_op jit(solution)/shard_map/while/body/eval_jaxpr/ppermute | solution.py:20
  467.3 12.5 %collective-permute-start.3 = (f32[192,1,128]{2,0,1:T(8,128)S(1)}, f32[192,1,128]{2,0,1:T(8,128)S(1)}, u32[]{:S(2)}, u32[]{:S(2)}) collective-permute-start(f32[192,1,128]{2,0,1:T(8,128)S(1)} %fusion.107), channel_id=1, source_target_pairs={{120,0},{0,8},{8,16},{16,24},{24,32},{32,40},{40,48},{48,56},{56,6... | collective-permute-start | bytes 294920 | tf_op jit(solution)/shard_map/while/body/eval_jaxpr/ppermute | solution.py:20
  469.5 12.5 %collective-permute-start.4 = (f32[192,1,128]{2,0,1:T(8,128)S(1)}, f32[192,1,128]{2,0,1:T(8,128)S(1)}, u32[]{:S(2)}, u32[]{:S(2)}) collective-permute-start(f32[192,1,128]{2,0,1:T(8,128)S(1)} %fusion.108), channel_id=1, source_target_pairs={{120,0},{0,8},{8,16},{16,24},{24,32},{32,40},{40,48},{48,56},{56,6... | collective-permute-start | bytes 294920 | tf_op jit(solution)/shard_map/while/body/eval_jaxpr/ppermute | solution.py:20
  482.1 15.3 %collective-permute-start = (bf16[192,1,128]{2,0,1:T(8,128)(2,1)S(1)}, bf16[192,1,128]{2,0,1:T(8,128)(2,1)S(1)}, u32[]{:S(2)}, u32[]{:S(2)}) collective-permute-start(bf16[192,1,128]{2,0,1:T(8,128)(2,1)S(1)} %copy.49), channel_id=1, source_target_pairs={{120,0},{0,8},{8,16},{16,24},{24,32},{32,40},{40,48},{48,56},{56,6... | collective-permute-start | bytes 147464 | tf_op jit(solution)/shard_map/while/body/eval_jaxpr/ppermute | solution.py:20
  484.0 13.4 %collective-permute-start.1 = (bf16[192,1,128]{2,0,1:T(8,128)(2,1)S(1)}, bf16[192,1,128]{2,0,1:T(8,128)(2,1)S(1)}, u32[]{:S(2)}, u32[]{:S(2)}) collective-permute-start(bf16[192,1,128]{2,0,1:T(8,128)(2,1)S(1)} %copy.50), channel_id=1, source_target_pairs={{120,0},{0,8},{8,16},{16,24},{24,32},{32,40},{40,48},{48,56},{56,6... | collective-permute-start | bytes 147464 | tf_op jit(solution)/shard_map/while/body/eval_jaxpr/ppermute | solution.py:20
  488.9 12.5 %collective-permute-start.3 = (f32[192,1,128]{2,0,1:T(8,128)S(1)}, f32[192,1,128]{2,0,1:T(8,128)S(1)}, u32[]{:S(2)}, u32[]{:S(2)}) collective-permute-start(f32[192,1,128]{2,0,1:T(8,128)S(1)} %fusion.107), channel_id=1, source_target_pairs={{120,0},{0,8},{8,16},{16,24},{24,32},{32,40},{40,48},{48,56},{56,6... | collective-permute-start | bytes 294920 | tf_op jit(solution)/shard_map/while/body/eval_jaxpr/ppermute | solution.py:20
  491.2 12.5 %collective-permute-start.4 = (f32[192,1,128]{2,0,1:T(8,128)S(1)}, f32[192,1,128]{2,0,1:T(8,128)S(1)}, u32[]{:S(2)}, u32[]{:S(2)}) collective-permute-start(f32[192,1,128]{2,0,1:T(8,128)S(1)} %fusion.108), channel_id=1, source_target_pairs={{120,0},{0,8},{8,16},{16,24},{24,32},{32,40},{40,48},{48,56},{56,6... | collective-permute-start | bytes 294920 | tf_op jit(solution)/shard_map/while/body/eval_jaxpr/ppermute | solution.py:20
  503.7 15.3 %collective-permute-start = (bf16[192,1,128]{2,0,1:T(8,128)(2,1)S(1)}, bf16[192,1,128]{2,0,1:T(8,128)(2,1)S(1)}, u32[]{:S(2)}, u32[]{:S(2)}) collective-permute-start(bf16[192,1,128]{2,0,1:T(8,128)(2,1)S(1)} %copy.49), channel_id=1, source_target_pairs={{120,0},{0,8},{8,16},{16,24},{24,32},{32,40},{40,48},{48,56},{56,6... | collective-permute-start | bytes 147464 | tf_op jit(solution)/shard_map/while/body/eval_jaxpr/ppermute | solution.py:20
  505.6 13.4 %collective-permute-start.1 = (bf16[192,1,128]{2,0,1:T(8,128)(2,1)S(1)}, bf16[192,1,128]{2,0,1:T(8,128)(2,1)S(1)}, u32[]{:S(2)}, u32[]{:S(2)}) collective-permute-start(bf16[192,1,128]{2,0,1:T(8,128)(2,1)S(1)} %copy.50), channel_id=1, source_target_pairs={{120,0},{0,8},{8,16},{16,24},{24,32},{32,40},{40,48},{48,56},{56,6... | collective-permute-start | bytes 147464 | tf_op jit(solution)/shard_map/while/body/eval_jaxpr/ppermute | solution.py:20
  525.3 15.3 %collective-permute-start = (bf16[192,1,128]{2,0,1:T(8,128)(2,1)S(1)}, bf16[192,1,128]{2,0,1:T(8,128)(2,1)S(1)}, u32[]{:S(2)}, u32[]{:S(2)}) collective-permute-start(bf16[192,1,128]{2,0,1:T(8,128)(2,1)S(1)} %copy.49), channel_id=1, source_target_pairs={{120,0},{0,8},{8,16},{16,24},{24,32},{32,40},{40,48},{48,56},{56,6... | collective-permute-start | bytes 147464 | tf_op jit(solution)/shard_map/while/body/eval_jaxpr/ppermute | solution.py:20
  527.3 13.4 %collective-permute-start.1 = (bf16[192,1,128]{2,0,1:T(8,128)(2,1)S(1)}, bf16[192,1,128]{2,0,1:T(8,128)(2,1)S(1)}, u32[]{:S(2)}, u32[]{:S(2)}) collective-permute-start(bf16[192,1,128]{2,0,1:T(8,128)(2,1)S(1)} %copy.50), channel_id=1, source_target_pairs={{120,0},{0,8},{8,16},{16,24},{24,32},{32,40},{40,48},{48,56},{56,6... | collective-permute-start | bytes 147464 | tf_op jit(solution)/shard_map/while/body/eval_jaxpr/ppermute | solution.py:20
  532.2 12.5 %collective-permute-start.3 = (f32[192,1,128]{2,0,1:T(8,128)S(1)}, f32[192,1,128]{2,0,1:T(8,128)S(1)}, u32[]{:S(2)}, u32[]{:S(2)}) collective-permute-start(f32[192,1,128]{2,0,1:T(8,128)S(1)} %fusion.107), channel_id=1, source_target_pairs={{120,0},{0,8},{8,16},{16,24},{24,32},{32,40},{40,48},{48,56},{56,6... | collective-permute-start | bytes 294920 | tf_op jit(solution)/shard_map/while/body/eval_jaxpr/ppermute | solution.py:20
  534.4 12.5 %collective-permute-start.4 = (f32[192,1,128]{2,0,1:T(8,128)S(1)}, f32[192,1,128]{2,0,1:T(8,128)S(1)}, u32[]{:S(2)}, u32[]{:S(2)}) collective-permute-start(f32[192,1,128]{2,0,1:T(8,128)S(1)} %fusion.108), channel_id=1, source_target_pairs={{120,0},{0,8},{8,16},{16,24},{24,32},{32,40},{40,48},{48,56},{56,6... | collective-permute-start | bytes 294920 | tf_op jit(solution)/shard_map/while/body/eval_jaxpr/ppermute | solution.py:20
  546.9 15.3 %collective-permute-start = (bf16[192,1,128]{2,0,1:T(8,128)(2,1)S(1)}, bf16[192,1,128]{2,0,1:T(8,128)(2,1)S(1)}, u32[]{:S(2)}, u32[]{:S(2)}) collective-permute-start(bf16[192,1,128]{2,0,1:T(8,128)(2,1)S(1)} %copy.49), channel_id=1, source_target_pairs={{120,0},{0,8},{8,16},{16,24},{24,32},{32,40},{40,48},{48,56},{56,6... | collective-permute-start | bytes 147464 | tf_op jit(solution)/shard_map/while/body/eval_jaxpr/ppermute | solution.py:20
  548.9 13.4 %collective-permute-start.1 = (bf16[192,1,128]{2,0,1:T(8,128)(2,1)S(1)}, bf16[192,1,128]{2,0,1:T(8,128)(2,1)S(1)}, u32[]{:S(2)}, u32[]{:S(2)}) collective-permute-start(bf16[192,1,128]{2,0,1:T(8,128)(2,1)S(1)} %copy.50), channel_id=1, source_target_pairs={{120,0},{0,8},{8,16},{16,24},{24,32},{32,40},{40,48},{48,56},{56,6... | collective-permute-start | bytes 147464 | tf_op jit(solution)/shard_map/while/body/eval_jaxpr/ppermute | solution.py:20
  556.0 12.5 %collective-permute-start.4 = (f32[192,1,128]{2,0,1:T(8,128)S(1)}, f32[192,1,128]{2,0,1:T(8,128)S(1)}, u32[]{:S(2)}, u32[]{:S(2)}) collective-permute-start(f32[192,1,128]{2,0,1:T(8,128)S(1)} %fusion.108), channel_id=1, source_target_pairs={{120,0},{0,8},{8,16},{16,24},{24,32},{32,40},{40,48},{48,56},{56,6... | collective-permute-start | bytes 294920 | tf_op jit(solution)/shard_map/while/body/eval_jaxpr/ppermute | solution.py:20
  (21 other events, 356.8 us)
Sparse Core Ops, SparseCore 0:
  10.2 129.0 all-gather.4
  577.0 439.2 reduce-scatter.3
